TPU v7x, 32 devices: a whole 2x2x4 slice. The times are simulated.
32 devices in a mesh: seq: 16 (over z, y, x), head: 2 (over core).
Axes of the slice: x: 2, y: 2, z: 4, core: 2. Of those that a mesh axis runs over, the one named last changes fastest.
Arguments:
- attn_q: bfloat16 [2048, 512], P('seq', 'head'), may hold values from -6 to 6
- attn_k: bfloat16 [2048, 512], P('seq', 'head'), may hold values from -6 to 6
- attn_v: bfloat16 [2048, 512], P('seq', 'head'), may hold values from -6 to 6
- attn_out: bfloat16 [2048, 512], P('seq', 'head'), may hold values from -0.29882812 to 0.29882812
- attn_dout: bfloat16 [2048, 512], P('seq', 'head'), may hold values from -96 to 96
- attn_lse: float32 [4, 2048], P('head', 'seq'), may hold values from 7 to 8
- w_kv: bfloat16 [512, 2, 512], P('seq', None, 'head'), may hold values from -0.25 to 0.25
- gdn_q: bfloat16 [2048, 512], P('seq', 'head'), may hold values from -6 to 6
- gdn_k: bfloat16 [2048, 512], P('seq', 'head'), may hold values from -6 to 6
- gdn_v: bfloat16 [2048, 512], P('seq', 'head'), may hold values from -6 to 6
- gdn_dout: bfloat16 [2048, 512], P('seq', 'head'), may hold values from -6 to 6
- gdn_log_decay: float32 [4, 2048], P('head', 'seq'), may hold values from -0.56 to 0
- gdn_beta: float32 [4, 2048], P('head', 'seq'), may hold values from 0 to 0.9
- gdn_states: float32 [32, 4, 128, 128], P('seq', 'head'), may hold values from -24 to 24
Outputs:
- attn_dq: bfloat16 [2048, 512], P('seq', 'head')
- attn_dx: bfloat16 [512, 2048], P('head', 'seq')
- gdn_dq: bfloat16 [2048, 512], P('seq', 'head')
- gdn_dk: bfloat16 [2048, 512], P('seq', 'head')
- gdn_dv: bfloat16 [2048, 512], P('seq', 'head')
- gdn_dlog_decay: float32 [4, 2048], P('head', 'seq')
- gdn_dbeta: float32 [4, 2048], P('head', 'seq')
All inputs are finite; a program needn't handle non-finite values.
Results may differ from a plain program's by a relative error of at most 0.0078.
Values may be sent and summed in bfloat16 or wider, within the bound.
A program may use at most 64 MiB of HBM per device.

v0:
```python
import jax
import jax.numpy as jnp
from jax import lax
from jax.sharding import PartitionSpec as P

BLOCK = 64
WINDOW = 1024
HIGH = lax.Precision.HIGHEST


def from_behind(block, axis, distance):
    devices = range(lax.axis_size(axis))
    route = [(i - distance, i) for i in devices if i - distance in devices]
    return lax.ppermute(block, axis, route)


def matmul(left_side, right_side):
    return jnp.dot(left_side, right_side, precision=HIGH)


def stack_mul(left_side, right_side):
    return jnp.einsum("hij,hjk->hik", left_side, right_side, precision=HIGH)


def unit_rows(matrix):
    return matrix * lax.rsqrt(jnp.sum(matrix * matrix, axis=-1, keepdims=True) + 1e-06)


def inverse_unit(lower_part):
    length = lower_part.shape[0]
    identity = jnp.eye(length, dtype=jnp.float32)
    powered = lower_part
    result = identity - lower_part
    for _ in range(length.bit_length() - 2):
        powered = matmul(powered, powered)
        result = matmul(result, identity + powered)
    return result


def block_parts(queries, keys_in, decays, strengths):
    length, depth = queries.shape
    unit_q = unit_rows(queries) * depth ** (-0.5)
    unit_k = unit_rows(keys_in)
    summed = jnp.cumsum(decays)
    row_ids = lax.broadcasted_iota(jnp.int32, (length, length), 0)
    col_ids = lax.broadcasted_iota(jnp.int32, (length, length), 1)
    causal = row_ids >= col_ids
    fading = jnp.where(
        causal, jnp.exp(jnp.where(causal, summed[:, None] - summed[None, :], 0.0)), 0.0
    )
    strict = jnp.where(row_ids > col_ids, fading, 0.0)
    lower_part = strengths[:, None] * strict * matmul(unit_k, unit_k.T)
    solved = inverse_unit(lower_part)
    growth = jnp.exp(summed)
    widened = matmul(solved, (strengths * growth)[:, None] * unit_k)
    attention = fading * matmul(unit_q, unit_k.T)
    tailing = jnp.exp(summed[-1] - summed)[:, None] * unit_k
    return (unit_q, solved, growth, widened, attention, tailing)


def block_forward(queries, keys_in, values, decays, strengths, initial):
    unit_q, solved, growth, widened, attention, tailing = block_parts(
        queries, keys_in, decays, strengths
    )
    fresh = matmul(solved, strengths[:, None] * values) - matmul(widened, initial)
    output = growth[:, None] * matmul(unit_q, initial) + matmul(attention, fresh)
    final = growth[-1] * initial + matmul(tailing.T, fresh)
    return (output, final)


def block_adjoint(queries, keys_in, decays, strengths, out_grad):
    unit_q, solved, growth, widened, attention, tailing = block_parts(
        queries, keys_in, decays, strengths
    )
    depth = queries.shape[1]
    carry_map = growth[-1] * jnp.eye(depth, dtype=jnp.float32) - matmul(widened.T, tailing)
    local_term = matmul((growth[:, None] * unit_q).T, out_grad) - matmul(
        widened.T, matmul(attention.T, out_grad)
    )
    return (carry_map, local_term)


def block_grads(queries, keys_in, values, decays, strengths, initial, out_grad, later_adjoint):
    _, pullback = jax.vjp(block_forward, queries, keys_in, values, decays, strengths, initial)
    grad_q, grad_k, grad_v, grad_decay, grad_beta, _ = pullback((out_grad, later_adjoint))
    return (grad_q, grad_k, grad_v, grad_decay, grad_beta)


def window_terms(queries, keys_in, values, out_grad, log_totals, dot_terms, query_pos, key_pos):
    scaling = queries.shape[2] ** (-0.5)
    logits = (
        jnp.einsum("rhd,khd->hrk", queries, keys_in, preferred_element_type=jnp.float32) * scaling
    )
    distance = query_pos[:, None] - key_pos[None, :]
    visible = ((distance >= 0) & (distance < WINDOW) & (key_pos[None, :] >= 0))[None, :, :]
    chances = jnp.where(
        visible, jnp.exp(jnp.where(visible, logits - log_totals[:, :, None], 0.0)), 0.0
    )
    grad_prob = jnp.einsum("rhd,khd->hrk", out_grad, values, preferred_element_type=jnp.float32)
    grad_logit = (chances * (grad_prob - dot_terms[:, :, None])).astype(jnp.bfloat16)
    weights = chances.astype(jnp.bfloat16)
    grad_q = (
        jnp.einsum("hrk,khd->rhd", grad_logit, keys_in, preferred_element_type=jnp.float32)
        * scaling
    )
    grad_k = (
        jnp.einsum("hrk,rhd->khd", grad_logit, queries, preferred_element_type=jnp.float32)
        * scaling
    )
    grad_v = jnp.einsum("hrk,rhd->khd", weights, out_grad, preferred_element_type=jnp.float32)
    return (grad_q, grad_k, grad_v)


def per_device(
    attn_q,
    attn_k,
    attn_v,
    attn_out,
    attn_dout,
    attn_lse,
    w_kv,
    gdn_q,
    gdn_k,
    gdn_v,
    gdn_dout,
    gdn_log_decay,
    gdn_beta,
    gdn_states,
):
    row_count, column_count = attn_q.shape
    head_count = attn_lse.shape[0]
    depth = column_count // head_count
    reach_count = WINDOW // row_count
    position = lax.axis_index("seq")

    def by_heads(matrix):
        return matrix.reshape(-1, head_count, depth)

    dot_terms = jnp.sum(
        by_heads(attn_dout).astype(jnp.float32) * by_heads(attn_out).astype(jnp.float32), axis=2
    ).T
    query_pos = position * row_count + jnp.arange(row_count, dtype=jnp.int32)
    couple = jnp.stack([attn_k, attn_v])
    pieces = []
    for offset_by in range(reach_count, 0, -1):
        pieces.append(from_behind(couple, "seq", offset_by))
    before = jnp.concatenate(pieces, axis=1)
    window = jnp.concatenate([before, couple], axis=1)
    key_pos = (position - reach_count) * row_count + jnp.arange(
        (reach_count + 1) * row_count, dtype=jnp.int32
    )
    grad_q, grad_k, grad_v = window_terms(
        by_heads(attn_q),
        by_heads(window[0]),
        by_heads(window[1]),
        by_heads(attn_dout),
        attn_lse,
        dot_terms,
        query_pos,
        key_pos,
    )
    own_rows = jnp.stack([attn_q, attn_dout])
    own_stats = jnp.stack([attn_lse, dot_terms])
    query_parts = [own_rows]
    stat_parts = [own_stats]
    for offset_by in range(1, reach_count + 1):
        query_parts.append(from_behind(own_rows, "seq", -offset_by))
        stat_parts.append(from_behind(own_stats, "seq", -offset_by))
    later_rows = jnp.concatenate(query_parts, axis=1)
    later_stats = jnp.concatenate(stat_parts, axis=2)
    later_pos = position * row_count + jnp.arange((reach_count + 1) * row_count, dtype=jnp.int32)
    _, own_k, own_v = window_terms(
        by_heads(later_rows[0]),
        by_heads(attn_k),
        by_heads(attn_v),
        by_heads(later_rows[1]),
        later_stats[0],
        later_stats[1],
        later_pos,
        query_pos,
    )
    key_grad = own_k.reshape(row_count, column_count).astype(jnp.bfloat16)
    value_grad = own_v.reshape(row_count, column_count).astype(jnp.bfloat16)
    attn_dq = grad_q.reshape(row_count, column_count).astype(jnp.bfloat16)
    row_piece = lax.all_gather(w_kv, "seq", axis=0, tiled=True)
    from_keys = lax.dot_general(
        row_piece[:, 0, :], key_grad, (((1,), (1,)), ((), ())), preferred_element_type=jnp.float32
    )
    partial_value = from_keys + lax.dot_general(
        row_piece[:, 1, :], value_grad, (((1,), (1,)), ((), ())), preferred_element_type=jnp.float32
    )
    attn_dx = lax.psum_scatter(partial_value, "head", scatter_dimension=0, tiled=True).astype(
        jnp.bfloat16
    )
    block_count = row_count // BLOCK

    def by_blocks(matrix):
        return (
            matrix.reshape(block_count, BLOCK, head_count, depth)
            .transpose(0, 2, 1, 3)
            .astype(jnp.float32)
        )

    def gates_by_blocks(matrix):
        return matrix.reshape(head_count, block_count, BLOCK).transpose(1, 0, 2)

    queries = by_blocks(gdn_q)
    keys_in = by_blocks(gdn_k)
    values = by_blocks(gdn_v)
    out_grad = by_blocks(gdn_dout)
    decays = gates_by_blocks(gdn_log_decay)
    strengths = gates_by_blocks(gdn_beta)
    carry_map, local_term = jax.vmap(jax.vmap(block_adjoint))(
        queries, keys_in, decays, strengths, out_grad
    )
    identity = jnp.broadcast_to(jnp.eye(depth, dtype=jnp.float32), (head_count, depth, depth))
    nothing = jnp.zeros((head_count, depth, depth), jnp.float32)

    def compose_blocks(carry, couple_in):
        across, offset = carry
        return (
            (stack_mul(couple_in[0], across), stack_mul(couple_in[0], offset) + couple_in[1]),
            None,
        )

    (across, offset), _ = lax.scan(
        compose_blocks, (identity, nothing), (carry_map, local_term), reverse=True
    )

    def relay_step(step_no, incoming):
        return from_behind(stack_mul(across, incoming) + offset, "seq", -1)

    carried = lax.fori_loop(0, lax.axis_size("seq") - 1, relay_step, nothing)

    def backward(carry, couple_in):
        return (stack_mul(couple_in[0], carry) + couple_in[1], carry)

    _, later_adjoint = lax.scan(backward, carried, (carry_map, local_term), reverse=True)
    grad_bq, grad_bk, grad_bv, grad_decay, grad_beta = jax.vmap(jax.vmap(block_grads))(
        queries, keys_in, values, decays, strengths, gdn_states, out_grad, later_adjoint
    )

    def tokens_back(stacked):
        return stacked.transpose(0, 2, 1, 3).reshape(row_count, column_count).astype(jnp.bfloat16)

    def per_head(stacked):
        return stacked.transpose(1, 0, 2).reshape(head_count, row_count)

    return (
        attn_dq,
        attn_dx,
        tokens_back(grad_bq),
        tokens_back(grad_bk),
        tokens_back(grad_bv),
        per_head(grad_decay),
        per_head(grad_beta),
    )


def solution(mesh):
    placed = (
        P("seq", "head"),
        P("seq", "head"),
        P("seq", "head"),
        P("seq", "head"),
        P("seq", "head"),
        P("head", "seq"),
        P("seq", None, "head"),
        P("seq", "head"),
        P("seq", "head"),
        P("seq", "head"),
        P("seq", "head"),
        P("head", "seq"),
        P("head", "seq"),
        P("seq", "head", None, None),
    )
    return jax.shard_map(
        per_device,
        mesh=mesh,
        in_specs=placed,
        out_specs=(
            P("seq", "head"),
            P("head", "seq"),
            P("seq", "head"),
            P("seq", "head"),
            P("seq", "head"),
            P("head", "seq"),
            P("head", "seq"),
        ),
        check_vma=False,
    )
```

profile of v0, /device:TPU:0, one launch (start us, length us, event | category | flops | bytes accessed | tf_op | source)
XLA Modules:
  0.0 311.4 jit_solution(4315394593394781818)
XLA Ops:
  11.3 1.3 collective-permute-start.18
  12.6 1.3 collective-permute-start.19
  13.9 1.3 collective-permute-start.20
  25.4 1.3 fusion.50
  30.9 133.4 %while.43 = (s32[]{:T(128)}, f32[2,128,128]{2,1,0:T(8,128)S(1)}, f32[2,128,128]{2,1,0:T(8,128)S(1)}, f32[2,128,128]{2,1,0:T(8,128)S(1)}, s32[]{:T(128)}) while((s32[]{:T(128)}, f32[2,128,128]{2,1,0:T(8,128)S(1)}, f32[2,128,128]{2,1,0:T(8,128)S(1)}, f32[2,128,128]{2,1,0:T(8,128)S(1)}, s32[]{:T(128)}) %tuple.116), condition=%wide.region_9.10_spmd, body=%wide.region_8.9_spmd.sunk | while | flops 50364416 | bytes 1048677 | solution.py:233
  31.2 1.3 collective-permute-start
  32.5 7.7 %collective-permute-done = f32[2,128,128]{2,1,0:T(8,128)S(1)} collective-permute-done((f32[2,128,128]{2,1,0:T(8,128)S(1)}, f32[2,128,128]{2,1,0:T(8,128)S(1)}, u32[]{:S(2)}, u32[]{:S(2)}) %collective-permute-start) | collective-permute-done | bytes 131104 | tf_op jit(solution)/shard_map/while/body/eval_jaxpr/ppermute | solution.py:14
  40.4 1.3 collective-permute-start
  41.8 6.8 %collective-permute-done = f32[2,128,128]{2,1,0:T(8,128)S(1)} collective-permute-done((f32[2,128,128]{2,1,0:T(8,128)S(1)}, f32[2,128,128]{2,1,0:T(8,128)S(1)}, u32[]{:S(2)}, u32[]{:S(2)}) %collective-permute-start) | collective-permute-done | bytes 131104 | tf_op jit(solution)/shard_map/while/body/eval_jaxpr/ppermute | solution.py:14
  48.8 1.3 collective-permute-start
  50.1 6.5 %collective-permute-done = f32[2,128,128]{2,1,0:T(8,128)S(1)} collective-permute-done((f32[2,128,128]{2,1,0:T(8,128)S(1)}, f32[2,128,128]{2,1,0:T(8,128)S(1)}, u32[]{:S(2)}, u32[]{:S(2)}) %collective-permute-start) | collective-permute-done | bytes 131104 | tf_op jit(solution)/shard_map/while/body/eval_jaxpr/ppermute | solution.py:14
  56.9 1.3 collective-permute-start
  58.2 6.5 %collective-permute-done = f32[2,128,128]{2,1,0:T(8,128)S(1)} collective-permute-done((f32[2,128,128]{2,1,0:T(8,128)S(1)}, f32[2,128,128]{2,1,0:T(8,128)S(1)}, u32[]{:S(2)}, u32[]{:S(2)}) %collective-permute-start) | collective-permute-done | bytes 131104 | tf_op jit(solution)/shard_map/while/body/eval_jaxpr/ppermute | solution.py:14
  64.9 1.3 collective-permute-start
  66.2 6.9 %collective-permute-done = f32[2,128,128]{2,1,0:T(8,128)S(1)} collective-permute-done((f32[2,128,128]{2,1,0:T(8,128)S(1)}, f32[2,128,128]{2,1,0:T(8,128)S(1)}, u32[]{:S(2)}, u32[]{:S(2)}) %collective-permute-start) | collective-permute-done | bytes 131104 | tf_op jit(solution)/shard_map/while/body/eval_jaxpr/ppermute | solution.py:14
  73.4 1.3 collective-permute-start
  74.7 7.4 %collective-permute-done = f32[2,128,128]{2,1,0:T(8,128)S(1)} collective-permute-done((f32[2,128,128]{2,1,0:T(8,128)S(1)}, f32[2,128,128]{2,1,0:T(8,128)S(1)}, u32[]{:S(2)}, u32[]{:S(2)}) %collective-permute-start) | collective-permute-done | bytes 131104 | tf_op jit(solution)/shard_map/while/body/eval_jaxpr/ppermute | solution.py:14
  82.3 1.3 collective-permute-start
  83.6 8.7 %collective-permute-done = f32[2,128,128]{2,1,0:T(8,128)S(1)} collective-permute-done((f32[2,128,128]{2,1,0:T(8,128)S(1)}, f32[2,128,128]{2,1,0:T(8,128)S(1)}, u32[]{:S(2)}, u32[]{:S(2)}) %collective-permute-start) | collective-permute-done | bytes 131104 | tf_op jit(solution)/shard_map/while/body/eval_jaxpr/ppermute | solution.py:14
  92.5 1.3 collective-permute-start
  93.8 8.7 %collective-permute-done = f32[2,128,128]{2,1,0:T(8,128)S(1)} collective-permute-done((f32[2,128,128]{2,1,0:T(8,128)S(1)}, f32[2,128,128]{2,1,0:T(8,128)S(1)}, u32[]{:S(2)}, u32[]{:S(2)}) %collective-permute-start) | collective-permute-done | bytes 131104 | tf_op jit(solution)/shard_map/while/body/eval_jaxpr/ppermute | solution.py:14
  102.9 1.3 collective-permute-start
  104.2 7.2 %collective-permute-done = f32[2,128,128]{2,1,0:T(8,128)S(1)} collective-permute-done((f32[2,128,128]{2,1,0:T(8,128)S(1)}, f32[2,128,128]{2,1,0:T(8,128)S(1)}, u32[]{:S(2)}, u32[]{:S(2)}) %collective-permute-start) | collective-permute-done | bytes 131104 | tf_op jit(solution)/shard_map/while/body/eval_jaxpr/ppermute | solution.py:14
  111.6 1.3 collective-permute-start
  112.9 6.8 %collective-permute-done = f32[2,128,128]{2,1,0:T(8,128)S(1)} collective-permute-done((f32[2,128,128]{2,1,0:T(8,128)S(1)}, f32[2,128,128]{2,1,0:T(8,128)S(1)}, u32[]{:S(2)}, u32[]{:S(2)}) %collective-permute-start) | collective-permute-done | bytes 131104 | tf_op jit(solution)/shard_map/while/body/eval_jaxpr/ppermute | solution.py:14
  120.0 1.3 collective-permute-start
  121.3 7.1 %collective-permute-done = f32[2,128,128]{2,1,0:T(8,128)S(1)} collective-permute-done((f32[2,128,128]{2,1,0:T(8,128)S(1)}, f32[2,128,128]{2,1,0:T(8,128)S(1)}, u32[]{:S(2)}, u32[]{:S(2)}) %collective-permute-start) | collective-permute-done | bytes 131104 | tf_op jit(solution)/shard_map/while/body/eval_jaxpr/ppermute | solution.py:14
  128.7 1.3 collective-permute-start
  130.0 7.4 %collective-permute-done = f32[2,128,128]{2,1,0:T(8,128)S(1)} collective-permute-done((f32[2,128,128]{2,1,0:T(8,128)S(1)}, f32[2,128,128]{2,1,0:T(8,128)S(1)}, u32[]{:S(2)}, u32[]{:S(2)}) %collective-permute-start) | collective-permute-done | bytes 131104 | tf_op jit(solution)/shard_map/while/body/eval_jaxpr/ppermute | solution.py:14
  137.6 1.3 collective-permute-start
  138.9 7.4 %collective-permute-done = f32[2,128,128]{2,1,0:T(8,128)S(1)} collective-permute-done((f32[2,128,128]{2,1,0:T(8,128)S(1)}, f32[2,128,128]{2,1,0:T(8,128)S(1)}, u32[]{:S(2)}, u32[]{:S(2)}) %collective-permute-start) | collective-permute-done | bytes 131104 | tf_op jit(solution)/shard_map/while/body/eval_jaxpr/ppermute | solution.py:14
  146.5 1.3 collective-permute-start
  147.8 7.4 %collective-permute-done = f32[2,128,128]{2,1,0:T(8,128)S(1)} collective-permute-done((f32[2,128,128]{2,1,0:T(8,128)S(1)}, f32[2,128,128]{2,1,0:T(8,128)S(1)}, u32[]{:S(2)}, u32[]{:S(2)}) %collective-permute-start) | collective-permute-done | bytes 131104 | tf_op jit(solution)/shard_map/while/body/eval_jaxpr/ppermute | solution.py:14
  156.8 7.5 %collective-permute-done = f32[2,128,128]{2,1,0:T(8,128)S(1)} collective-permute-done((f32[2,128,128]{2,1,0:T(8,128)S(1)}, f32[2,128,128]{2,1,0:T(8,128)S(1)}, u32[]{:S(2)}, u32[]{:S(2)}) %collective-permute-start) | collective-permute-done | bytes 131104 | tf_op jit(solution)/shard_map/while/body/eval_jaxpr/ppermute | solution.py:14
  164.3 1.5 collective-permute-start.21
  180.5 54.2 %all_gather.3 = bf16[512,2,256]{2,0,1:T(8,128)(2,1)S(1)} all-gather(bf16[32,2,256]{2,0,1:T(8,128)(2,1)S(1)} %copy.284), channel_id=1, replica_groups=mesh['seq'=16,'head'=2] {'seq'}, dimensions={0}, use_global_device_ids=true | all-gather | bytes 557056 | tf_op jit(solution)/shard_map/all_gather | solution.py:185
  236.6 1.4 fusion.41
  242.9 1.3 collective-permute-start.22
  244.3 1.5 collective-permute-start.23
  257.5 1.9 collective-permute-done.11
  260.7 10.6 %collective-permute-start.1 = (bf16[2,128,256]{1,2,0:T(8,128)(2,1)S(1)}, bf16[2,128,256]{1,2,0:T(8,128)(2,1)}, u32[]{:S(2)}, u32[]{:S(2)}) collective-permute-start(bf16[2,128,256]{1,2,0:T(8,128)(2,1)S(1)} %pad_maximum_fusion), channel_id=1, source_target_pairs={{0,16},{2,18},{4,20},{6,22},{8,24},{10,26},{12,28},{14,30},{1,17},... | collective-permute-start | bytes 393224 | tf_op jit(solution)/shard_map/ppermute | solution.py:14
  271.3 6.4 %collective-permute-start.2 = (bf16[2,128,256]{1,2,0:T(8,128)(2,1)S(1)}, bf16[2,128,256]{1,2,0:T(8,128)(2,1)}, u32[]{:S(2)}, u32[]{:S(2)}) collective-permute-start(bf16[2,128,256]{1,2,0:T(8,128)(2,1)S(1)} %pad_maximum_fusion), channel_id=1, source_target_pairs={{0,14},{2,16},{4,18},{6,20},{8,22},{10,24},{12,26},{14,28},{16,30}... | collective-permute-start | bytes 393224 | tf_op jit(solution)/shard_map/ppermute | solution.py:14
  277.7 1.9 collective-permute-start.3
  279.7 2.0 collective-permute-start.4
  281.7 1.9 collective-permute-start.5
  287.8 3.0 collective-permute-start.6
  291.8 1.3 collective-permute-start.7
  294.0 3.1 collective-permute-start.8
  (291 shorter events, 72.3 us)
Async XLA Ops:
  7.2 295.8 %reduce-scatter.2.cloned.1.call-start = ((), (), s32[]{:S(2)}) async-start(), calls=%async_computation.1 | async-start | bytes 393216 | tf_op jit(solution)/shard_map/reduce_scatter | solution.py:192
  9.2 10.9 %copy-start.13 = (f32[128,2]{1,0:T(8,128)}, f32[128,2]{1,0:T(8,128)S(1)}, u32[]{:S(2)}) copy-start(f32[128,2]{1,0:T(8,128)S(1)} %multiply_reduce_fusion.4) | copy-start | bytes 3076
  10.0 232.9 %collective-permute-start.17 = (f32[2,2,128]{2,1,0:T(2,128)S(1)}, f32[2,2,128]{2,1,0:T(2,128)S(1)}, u32[]{:S(2)}, u32[]{:S(2)}) collective-permute-start(f32[2,2,128]{2,1,0:T(2,128)S(1)} %get-tuple-element.350), channel_id=1, source_target_pairs={{2,0},{4,2},{6,4},{8,6},{10,8},{12,10},{14,12},{16,14},{18,16},{20... | collective-permute-start | bytes 6152 | tf_op jit(solution)/shard_map/ppermute | solution.py:14
  11.3 233.0 %collective-permute-start.18 = (f32[2,2,128]{2,1,0:T(2,128)S(1)}, f32[2,2,128]{2,1,0:T(2,128)S(1)}, u32[]{:S(2)}, u32[]{:S(2)}) collective-permute-start(f32[2,2,128]{2,1,0:T(2,128)S(1)} %get-tuple-element.350), channel_id=1, source_target_pairs={{4,0},{6,2},{8,4},{10,6},{12,8},{14,10},{16,12},{18,14},{20,16},{2... | collective-permute-start | bytes 6152 | tf_op jit(solution)/shard_map/ppermute | solution.py:14
  12.6 233.2 %collective-permute-start.19 = (f32[2,2,128]{2,1,0:T(2,128)S(1)}, f32[2,2,128]{2,1,0:T(2,128)S(1)}, u32[]{:S(2)}, u32[]{:S(2)}) collective-permute-start(f32[2,2,128]{2,1,0:T(2,128)S(1)} %get-tuple-element.350), channel_id=1, source_target_pairs={{6,0},{8,2},{10,4},{12,6},{14,8},{16,10},{18,12},{20,14},{22,16},{... | collective-permute-start | bytes 6152 | tf_op jit(solution)/shard_map/ppermute | solution.py:14
  13.9 233.2 %collective-permute-start.20 = (f32[2,2,128]{2,1,0:T(2,128)S(1)}, f32[2,2,128]{2,1,0:T(2,128)S(1)}, u32[]{:S(2)}, u32[]{:S(2)}) collective-permute-start(f32[2,2,128]{2,1,0:T(2,128)S(1)} %get-tuple-element.350), channel_id=1, source_target_pairs={{8,0},{10,2},{12,4},{14,6},{16,8},{18,10},{20,12},{22,14},{24,16},... | collective-permute-start | bytes 6152 | tf_op jit(solution)/shard_map/ppermute | solution.py:14
  20.2 2.3 copy-start.2
  21.6 2.4 copy-start.25
  31.2 9.0 %collective-permute-start = (f32[2,128,128]{2,1,0:T(8,128)S(1)}, f32[2,128,128]{2,1,0:T(8,128)S(1)}, u32[]{:S(2)}, u32[]{:S(2)}) collective-permute-start(f32[2,128,128]{2,1,0:T(8,128)S(1)} %convolution_add_fusion.20), channel_id=1, source_target_pairs={{2,0},{4,2},{6,4},{8,6},{10,8},{12,10},{14,12},{16,14},{18,16},{20... | collective-permute-start | bytes 393224 | tf_op jit(solution)/shard_map/while/body/eval_jaxpr/ppermute | solution.py:14
  40.4 8.1 %collective-permute-start = (f32[2,128,128]{2,1,0:T(8,128)S(1)}, f32[2,128,128]{2,1,0:T(8,128)S(1)}, u32[]{:S(2)}, u32[]{:S(2)}) collective-permute-start(f32[2,128,128]{2,1,0:T(8,128)S(1)} %convolution_add_fusion.20), channel_id=1, source_target_pairs={{2,0},{4,2},{6,4},{8,6},{10,8},{12,10},{14,12},{16,14},{18,16},{20... | collective-permute-start | bytes 393224 | tf_op jit(solution)/shard_map/while/body/eval_jaxpr/ppermute | solution.py:14
  48.8 7.8 %collective-permute-start = (f32[2,128,128]{2,1,0:T(8,128)S(1)}, f32[2,128,128]{2,1,0:T(8,128)S(1)}, u32[]{:S(2)}, u32[]{:S(2)}) collective-permute-start(f32[2,128,128]{2,1,0:T(8,128)S(1)} %convolution_add_fusion.20), channel_id=1, source_target_pairs={{2,0},{4,2},{6,4},{8,6},{10,8},{12,10},{14,12},{16,14},{18,16},{20... | collective-permute-start | bytes 393224 | tf_op jit(solution)/shard_map/while/body/eval_jaxpr/ppermute | solution.py:14
  56.9 7.8 %collective-permute-start = (f32[2,128,128]{2,1,0:T(8,128)S(1)}, f32[2,128,128]{2,1,0:T(8,128)S(1)}, u32[]{:S(2)}, u32[]{:S(2)}) collective-permute-start(f32[2,128,128]{2,1,0:T(8,128)S(1)} %convolution_add_fusion.20), channel_id=1, source_target_pairs={{2,0},{4,2},{6,4},{8,6},{10,8},{12,10},{14,12},{16,14},{18,16},{20... | collective-permute-start | bytes 393224 | tf_op jit(solution)/shard_map/while/body/eval_jaxpr/ppermute | solution.py:14
  64.9 8.2 %collective-permute-start = (f32[2,128,128]{2,1,0:T(8,128)S(1)}, f32[2,128,128]{2,1,0:T(8,128)S(1)}, u32[]{:S(2)}, u32[]{:S(2)}) collective-permute-start(f32[2,128,128]{2,1,0:T(8,128)S(1)} %convolution_add_fusion.20), channel_id=1, source_target_pairs={{2,0},{4,2},{6,4},{8,6},{10,8},{12,10},{14,12},{16,14},{18,16},{20... | collective-permute-start | bytes 393224 | tf_op jit(solution)/shard_map/while/body/eval_jaxpr/ppermute | solution.py:14
  73.4 8.7 %collective-permute-start = (f32[2,128,128]{2,1,0:T(8,128)S(1)}, f32[2,128,128]{2,1,0:T(8,128)S(1)}, u32[]{:S(2)}, u32[]{:S(2)}) collective-permute-start(f32[2,128,128]{2,1,0:T(8,128)S(1)} %convolution_add_fusion.20), channel_id=1, source_target_pairs={{2,0},{4,2},{6,4},{8,6},{10,8},{12,10},{14,12},{16,14},{18,16},{20... | collective-permute-start | bytes 393224 | tf_op jit(solution)/shard_map/while/body/eval_jaxpr/ppermute | solution.py:14
  82.3 10.0 %collective-permute-start = (f32[2,128,128]{2,1,0:T(8,128)S(1)}, f32[2,128,128]{2,1,0:T(8,128)S(1)}, u32[]{:S(2)}, u32[]{:S(2)}) collective-permute-start(f32[2,128,128]{2,1,0:T(8,128)S(1)} %convolution_add_fusion.20), channel_id=1, source_target_pairs={{2,0},{4,2},{6,4},{8,6},{10,8},{12,10},{14,12},{16,14},{18,16},{20... | collective-permute-start | bytes 393224 | tf_op jit(solution)/shard_map/while/body/eval_jaxpr/ppermute | solution.py:14
  92.5 10.0 %collective-permute-start = (f32[2,128,128]{2,1,0:T(8,128)S(1)}, f32[2,128,128]{2,1,0:T(8,128)S(1)}, u32[]{:S(2)}, u32[]{:S(2)}) collective-permute-start(f32[2,128,128]{2,1,0:T(8,128)S(1)} %convolution_add_fusion.20), channel_id=1, source_target_pairs={{2,0},{4,2},{6,4},{8,6},{10,8},{12,10},{14,12},{16,14},{18,16},{20... | collective-permute-start | bytes 393224 | tf_op jit(solution)/shard_map/while/body/eval_jaxpr/ppermute | solution.py:14
  102.9 8.5 %collective-permute-start = (f32[2,128,128]{2,1,0:T(8,128)S(1)}, f32[2,128,128]{2,1,0:T(8,128)S(1)}, u32[]{:S(2)}, u32[]{:S(2)}) collective-permute-start(f32[2,128,128]{2,1,0:T(8,128)S(1)} %convolution_add_fusion.20), channel_id=1, source_target_pairs={{2,0},{4,2},{6,4},{8,6},{10,8},{12,10},{14,12},{16,14},{18,16},{20... | collective-permute-start | bytes 393224 | tf_op jit(solution)/shard_map/while/body/eval_jaxpr/ppermute | solution.py:14
  111.6 8.1 %collective-permute-start = (f32[2,128,128]{2,1,0:T(8,128)S(1)}, f32[2,128,128]{2,1,0:T(8,128)S(1)}, u32[]{:S(2)}, u32[]{:S(2)}) collective-permute-start(f32[2,128,128]{2,1,0:T(8,128)S(1)} %convolution_add_fusion.20), channel_id=1, source_target_pairs={{2,0},{4,2},{6,4},{8,6},{10,8},{12,10},{14,12},{16,14},{18,16},{20... | collective-permute-start | bytes 393224 | tf_op jit(solution)/shard_map/while/body/eval_jaxpr/ppermute | solution.py:14
  120.0 8.4 %collective-permute-start = (f32[2,128,128]{2,1,0:T(8,128)S(1)}, f32[2,128,128]{2,1,0:T(8,128)S(1)}, u32[]{:S(2)}, u32[]{:S(2)}) collective-permute-start(f32[2,128,128]{2,1,0:T(8,128)S(1)} %convolution_add_fusion.20), channel_id=1, source_target_pairs={{2,0},{4,2},{6,4},{8,6},{10,8},{12,10},{14,12},{16,14},{18,16},{20... | collective-permute-start | bytes 393224 | tf_op jit(solution)/shard_map/while/body/eval_jaxpr/ppermute | solution.py:14
  128.7 8.7 %collective-permute-start = (f32[2,128,128]{2,1,0:T(8,128)S(1)}, f32[2,128,128]{2,1,0:T(8,128)S(1)}, u32[]{:S(2)}, u32[]{:S(2)}) collective-permute-start(f32[2,128,128]{2,1,0:T(8,128)S(1)} %convolution_add_fusion.20), channel_id=1, source_target_pairs={{2,0},{4,2},{6,4},{8,6},{10,8},{12,10},{14,12},{16,14},{18,16},{20... | collective-permute-start | bytes 393224 | tf_op jit(solution)/shard_map/while/body/eval_jaxpr/ppermute | solution.py:14
  137.6 8.7 %collective-permute-start = (f32[2,128,128]{2,1,0:T(8,128)S(1)}, f32[2,128,128]{2,1,0:T(8,128)S(1)}, u32[]{:S(2)}, u32[]{:S(2)}) collective-permute-start(f32[2,128,128]{2,1,0:T(8,128)S(1)} %convolution_add_fusion.20), channel_id=1, source_target_pairs={{2,0},{4,2},{6,4},{8,6},{10,8},{12,10},{14,12},{16,14},{18,16},{20... | collective-permute-start | bytes 393224 | tf_op jit(solution)/shard_map/while/body/eval_jaxpr/ppermute | solution.py:14
  146.5 8.7 %collective-permute-start = (f32[2,128,128]{2,1,0:T(8,128)S(1)}, f32[2,128,128]{2,1,0:T(8,128)S(1)}, u32[]{:S(2)}, u32[]{:S(2)}) collective-permute-start(f32[2,128,128]{2,1,0:T(8,128)S(1)} %convolution_add_fusion.20), channel_id=1, source_target_pairs={{2,0},{4,2},{6,4},{8,6},{10,8},{12,10},{14,12},{16,14},{18,16},{20... | collective-permute-start | bytes 393224 | tf_op jit(solution)/shard_map/while/body/eval_jaxpr/ppermute | solution.py:14
  155.5 8.8 %collective-permute-start = (f32[2,128,128]{2,1,0:T(8,128)S(1)}, f32[2,128,128]{2,1,0:T(8,128)S(1)}, u32[]{:S(2)}, u32[]{:S(2)}) collective-permute-start(f32[2,128,128]{2,1,0:T(8,128)S(1)} %convolution_add_fusion.20), channel_id=1, source_target_pairs={{2,0},{4,2},{6,4},{8,6},{10,8},{12,10},{14,12},{16,14},{18,16},{20... | collective-permute-start | bytes 393224 | tf_op jit(solution)/shard_map/while/body/eval_jaxpr/ppermute | solution.py:14
  164.3 84.2 %collective-permute-start.21 = (f32[2,2,128]{2,1,0:T(2,128)S(1)}, f32[2,2,128]{2,1,0:T(2,128)S(1)}, u32[]{:S(2)}, u32[]{:S(2)}) collective-permute-start(f32[2,2,128]{2,1,0:T(2,128)S(1)} %get-tuple-element.350), channel_id=1, source_target_pairs={{10,0},{12,2},{14,4},{16,6},{18,8},{20,10},{22,12},{24,14},{26,16}... | collective-permute-start | bytes 6152 | tf_op jit(solution)/shard_map/ppermute | solution.py:14
  179.0 55.7 %copy-start.26 = (bf16[128,256]{1,0:T(8,128)(2,1)S(1)}, bf16[128,256]{1,0:T(8,128)(2,1)}, u32[]{:S(2)}) copy-start(bf16[128,256]{1,0:T(8,128)(2,1)} %param.21) | copy-start | bytes 196612
  179.2 55.7 %copy-start.20 = (bf16[128,256]{1,0:T(8,128)(2,1)S(1)}, bf16[128,256]{1,0:T(8,128)(2,1)}, u32[]{:S(2)}) copy-start(bf16[128,256]{1,0:T(8,128)(2,1)} %param.22) | copy-start | bytes 196612
  179.9 58.1 %copy-start.19 = (f32[2,2,64,128]{3,2,1,0:T(8,128)S(1)}, f32[2,2,64,128]{3,2,1,0:T(8,128)}, u32[]{:S(2)}) copy-start(f32[2,2,64,128]{3,2,1,0:T(8,128)} %get-tuple-element.352) | copy-start | bytes 393220
  238.0 4.8 %copy-start.14 = (f32[128,2]{1,0:T(8,128)S(1)}, f32[128,2]{1,0:T(8,128)}, u32[]{:S(2)}) copy-start(f32[128,2]{1,0:T(8,128)} %copy-done.13) | copy-start | bytes 3076
  238.2 17.9 %copy-start.1 = (bf16[2,1152,256]{1,2,0:T(8,128)(2,1)S(1)}, bf16[2,1152,256]{1,2,0:T(8,128)(2,1)}, u32[]{:S(2)}) copy-start(bf16[2,1152,256]{1,2,0:T(8,128)(2,1)} %get-tuple-element.335) | copy-start | bytes 3538948
  242.9 6.8 %collective-permute-start.22 = (f32[2,2,128]{2,1,0:T(2,128)S(1)}, f32[2,2,128]{2,1,0:T(2,128)S(1)}, u32[]{:S(2)}, u32[]{:S(2)}) collective-permute-start(f32[2,2,128]{2,1,0:T(2,128)S(1)} %get-tuple-element.350), channel_id=1, source_target_pairs={{12,0},{14,2},{16,4},{18,6},{20,8},{22,10},{24,12},{26,14},{28,16}... | collective-permute-start | bytes 6152 | tf_op jit(solution)/shard_map/ppermute | solution.py:14
  244.3 7.3 %collective-permute-start.23 = (f32[2,2,128]{2,1,0:T(2,128)S(1)}, f32[2,2,128]{2,1,0:T(2,128)S(1)}, u32[]{:S(2)}, u32[]{:S(2)}) collective-permute-start(f32[2,2,128]{2,1,0:T(2,128)S(1)} %get-tuple-element.350), channel_id=1, source_target_pairs={{14,0},{16,2},{18,4},{20,6},{22,8},{24,10},{26,12},{28,14},{30,16}... | collective-permute-start | bytes 6152 | tf_op jit(solution)/shard_map/ppermute | solution.py:14
  245.8 7.0 %collective-permute-start.24 = (f32[2,2,128]{2,1,0:T(2,128)S(1)}, f32[2,2,128]{2,1,0:T(2,128)S(1)}, u32[]{:S(2)}, u32[]{:S(2)}) collective-permute-start(f32[2,2,128]{2,1,0:T(2,128)S(1)} %get-tuple-element.350), channel_id=1, source_target_pairs={{16,0},{18,2},{20,4},{22,6},{24,8},{26,10},{28,12},{30,14},{17,1},... | collective-permute-start | bytes 6152 | tf_op jit(solution)/shard_map/ppermute | solution.py:14
  247.1 7.6 %collective-permute-start.9 = (bf16[2,128,256]{1,2,0:T(8,128)(2,1)S(1)}, bf16[2,128,256]{1,2,0:T(8,128)(2,1)S(1)}, u32[]{:S(2)}, u32[]{:S(2)}) collective-permute-start(bf16[2,128,256]{1,2,0:T(8,128)(2,1)S(1)} %get-tuple-element.334), channel_id=1, source_target_pairs={{2,0},{4,2},{6,4},{8,6},{10,8},{12,10},{14,12},{16,14},{18,16},{20... | collective-permute-start | bytes 393224 | tf_op jit(solution)/shard_map/ppermute | solution.py:14
  248.4 7.7 %collective-permute-start.10 = (bf16[2,128,256]{1,2,0:T(8,128)(2,1)S(1)}, bf16[2,128,256]{1,2,0:T(8,128)(2,1)S(1)}, u32[]{:S(2)}, u32[]{:S(2)}) collective-permute-start(bf16[2,128,256]{1,2,0:T(8,128)(2,1)S(1)} %get-tuple-element.334), channel_id=1, source_target_pairs={{4,0},{6,2},{8,4},{10,6},{12,8},{14,10},{16,12},{18,14},{20,16},{2... | collective-permute-start | bytes 393224 | tf_op jit(solution)/shard_map/ppermute | solution.py:14
  249.8 9.6 %collective-permute-start.11 = (bf16[2,128,256]{1,2,0:T(8,128)(2,1)S(1)}, bf16[2,128,256]{1,2,0:T(8,128)(2,1)S(1)}, u32[]{:S(2)}, u32[]{:S(2)}) collective-permute-start(bf16[2,128,256]{1,2,0:T(8,128)(2,1)S(1)} %get-tuple-element.334), channel_id=1, source_target_pairs={{6,0},{8,2},{10,4},{12,6},{14,8},{16,10},{18,12},{20,14},{22,16},{... | collective-permute-start | bytes 393224 | tf_op jit(solution)/shard_map/ppermute | solution.py:14
  251.5 9.1 %collective-permute-start.12 = (bf16[2,128,256]{1,2,0:T(8,128)(2,1)S(1)}, bf16[2,128,256]{1,2,0:T(8,128)(2,1)S(1)}, u32[]{:S(2)}, u32[]{:S(2)}) collective-permute-start(bf16[2,128,256]{1,2,0:T(8,128)(2,1)S(1)} %get-tuple-element.334), channel_id=1, source_target_pairs={{8,0},{10,2},{12,4},{14,6},{16,8},{18,10},{20,12},{22,14},{24,16},... | collective-permute-start | bytes 393224 | tf_op jit(solution)/shard_map/ppermute | solution.py:14
  252.8 18.4 %collective-permute-start.13 = (bf16[2,128,256]{1,2,0:T(8,128)(2,1)S(1)}, bf16[2,128,256]{1,2,0:T(8,128)(2,1)S(1)}, u32[]{:S(2)}, u32[]{:S(2)}) collective-permute-start(bf16[2,128,256]{1,2,0:T(8,128)(2,1)S(1)} %get-tuple-element.334), channel_id=1, source_target_pairs={{10,0},{12,2},{14,4},{16,6},{18,8},{20,10},{22,12},{24,14},{26,16}... | collective-permute-start | bytes 393224 | tf_op jit(solution)/shard_map/ppermute | solution.py:14
  254.8 22.9 %collective-permute-start.14 = (bf16[2,128,256]{1,2,0:T(8,128)(2,1)S(1)}, bf16[2,128,256]{1,2,0:T(8,128)(2,1)S(1)}, u32[]{:S(2)}, u32[]{:S(2)}) collective-permute-start(bf16[2,128,256]{1,2,0:T(8,128)(2,1)S(1)} %get-tuple-element.334), channel_id=1, source_target_pairs={{12,0},{14,2},{16,4},{18,6},{20,8},{22,10},{24,12},{26,14},{28,16}... | collective-permute-start | bytes 393224 | tf_op jit(solution)/shard_map/ppermute | solution.py:14
  256.1 23.6 %collective-permute-start.15 = (bf16[2,128,256]{1,2,0:T(8,128)(2,1)S(1)}, bf16[2,128,256]{1,2,0:T(8,128)(2,1)S(1)}, u32[]{:S(2)}, u32[]{:S(2)}) collective-permute-start(bf16[2,128,256]{1,2,0:T(8,128)(2,1)S(1)} %get-tuple-element.334), channel_id=1, source_target_pairs={{14,0},{16,2},{18,4},{20,6},{22,8},{24,10},{26,12},{28,14},{30,16}... | collective-permute-start | bytes 393224 | tf_op jit(solution)/shard_map/ppermute | solution.py:14
  259.3 22.4 %collective-permute-start.16 = (bf16[2,128,256]{1,2,0:T(8,128)(2,1)S(1)}, bf16[2,128,256]{1,2,0:T(8,128)(2,1)S(1)}, u32[]{:S(2)}, u32[]{:S(2)}) collective-permute-start(bf16[2,128,256]{1,2,0:T(8,128)(2,1)S(1)} %get-tuple-element.334), channel_id=1, source_target_pairs={{16,0},{18,2},{20,4},{22,6},{24,8},{26,10},{28,12},{30,14},{17,1},... | collective-permute-start | bytes 393224 | tf_op jit(solution)/shard_map/ppermute | solution.py:14
  260.7 27.2 %collective-permute-start.1 = (bf16[2,128,256]{1,2,0:T(8,128)(2,1)S(1)}, bf16[2,128,256]{1,2,0:T(8,128)(2,1)}, u32[]{:S(2)}, u32[]{:S(2)}) collective-permute-start(bf16[2,128,256]{1,2,0:T(8,128)(2,1)S(1)} %pad_maximum_fusion), channel_id=1, source_target_pairs={{0,16},{2,18},{4,20},{6,22},{8,24},{10,26},{12,28},{14,30},{1,17},... | collective-permute-start | bytes 393224 | tf_op jit(solution)/shard_map/ppermute | solution.py:14
  271.3 20.5 %collective-permute-start.2 = (bf16[2,128,256]{1,2,0:T(8,128)(2,1)S(1)}, bf16[2,128,256]{1,2,0:T(8,128)(2,1)}, u32[]{:S(2)}, u32[]{:S(2)}) collective-permute-start(bf16[2,128,256]{1,2,0:T(8,128)(2,1)S(1)} %pad_maximum_fusion), channel_id=1, source_target_pairs={{0,14},{2,16},{4,18},{6,20},{8,22},{10,24},{12,26},{14,28},{16,30}... | collective-permute-start | bytes 393224 | tf_op jit(solution)/shard_map/ppermute | solution.py:14
  277.7 16.3 %collective-permute-start.3 = (bf16[2,128,256]{1,2,0:T(8,128)(2,1)S(1)}, bf16[2,128,256]{1,2,0:T(8,128)(2,1)}, u32[]{:S(2)}, u32[]{:S(2)}) collective-permute-start(bf16[2,128,256]{1,2,0:T(8,128)(2,1)S(1)} %pad_maximum_fusion), channel_id=1, source_target_pairs={{0,12},{2,14},{4,16},{6,18},{8,20},{10,22},{12,24},{14,26},{16,28}... | collective-permute-start | bytes 393224 | tf_op jit(solution)/shard_map/ppermute | solution.py:14
  279.7 18.4 %collective-permute-start.4 = (bf16[2,128,256]{1,2,0:T(8,128)(2,1)S(1)}, bf16[2,128,256]{1,2,0:T(8,128)(2,1)}, u32[]{:S(2)}, u32[]{:S(2)}) collective-permute-start(bf16[2,128,256]{1,2,0:T(8,128)(2,1)S(1)} %pad_maximum_fusion), channel_id=1, source_target_pairs={{0,10},{2,12},{4,14},{6,16},{8,18},{10,20},{12,22},{14,24},{16,26}... | collective-permute-start | bytes 393224 | tf_op jit(solution)/shard_map/ppermute | solution.py:14
  281.7 17.3 %collective-permute-start.5 = (bf16[2,128,256]{1,2,0:T(8,128)(2,1)S(1)}, bf16[2,128,256]{1,2,0:T(8,128)(2,1)}, u32[]{:S(2)}, u32[]{:S(2)}) collective-permute-start(bf16[2,128,256]{1,2,0:T(8,128)(2,1)S(1)} %pad_maximum_fusion), channel_id=1, source_target_pairs={{0,8},{2,10},{4,12},{6,14},{8,16},{10,18},{12,20},{14,22},{16,24},... | collective-permute-start | bytes 393224 | tf_op jit(solution)/shard_map/ppermute | solution.py:14
  287.8 12.1 %collective-permute-start.6 = (bf16[2,128,256]{1,2,0:T(8,128)(2,1)S(1)}, bf16[2,128,256]{1,2,0:T(8,128)(2,1)S(1)}, u32[]{:S(2)}, u32[]{:S(2)}) collective-permute-start(bf16[2,128,256]{1,2,0:T(8,128)(2,1)S(1)} %pad_maximum_fusion), channel_id=1, source_target_pairs={{0,6},{2,8},{4,10},{6,12},{8,14},{10,16},{12,18},{14,20},{16,22},{... | collective-permute-start | bytes 393224 | tf_op jit(solution)/shard_map/ppermute | solution.py:14
  291.8 8.3 %collective-permute-start.7 = (bf16[2,128,256]{1,2,0:T(8,128)(2,1)S(1)}, bf16[2,128,256]{1,2,0:T(8,128)(2,1)S(1)}, u32[]{:S(2)}, u32[]{:S(2)}) collective-permute-start(bf16[2,128,256]{1,2,0:T(8,128)(2,1)S(1)} %pad_maximum_fusion), channel_id=1, source_target_pairs={{0,4},{2,6},{4,8},{6,10},{8,12},{10,14},{12,16},{14,18},{16,20},{1... | collective-permute-start | bytes 393224 | tf_op jit(solution)/shard_map/ppermute | solution.py:14
  294.0 6.1 %collective-permute-start.8 = (bf16[2,128,256]{1,2,0:T(8,128)(2,1)S(1)}, bf16[2,128,256]{1,2,0:T(8,128)(2,1)S(1)}, u32[]{:S(2)}, u32[]{:S(2)}) collective-permute-start(bf16[2,128,256]{1,2,0:T(8,128)(2,1)S(1)} %pad_maximum_fusion), channel_id=1, source_target_pairs={{0,2},{2,4},{4,6},{6,8},{8,10},{10,12},{12,14},{14,16},{16,18},{18... | collective-permute-start | bytes 393224 | tf_op jit(solution)/shard_map/ppermute | solution.py:14
  (25 other events, 38.0 us)
Sparse Core Ops, SparseCore 0:
  288.0 4.5 reduce-scatter.1
where the time goes:
time: 313 us; the launch traced here: 311 us
  waiting for transfers between devices  112 us (36%)
  starting transfers between devices  70.6 us (23%)
  blocking collectives  54.2 us (17%)
  matrix products  31.3 us (10%)
  local copies, waits for them, and re-layouts  19.6 us (6%)
  between operations  15.6 us (5%)
  other arithmetic  7.44 us (2%)
    ppermute x39, waiting for transfers between devices, from_behind(): return lax.ppermute(block, axis, route)  112 us
    ppermute x39, starting transfers between devices, from_behind(): return lax.ppermute(block, axis, route)  70.6 us
    all_gather x1, blocking collectives, per_device(): row_piece = lax.all_gather(w_kv, 'seq', axis=0, tiled=True)  54.2 us
    dot_general x53, matrix products, matmul(): return jnp.dot(left_side, right_side, precision=HIGH)  21.9 us
    unnamed x98, local copies, waits for them, and re-layouts  11.8 us
  transfers between devices with their start and end apart: 40, of which 17 were waited for; matrix products, arithmetic and copies ran while one was open for 16% of the time, Pallas kernels for 0%

commit v1 on v0

--- a/solution.py
+++ b/solution.py
@@ -182,7 +182,19 @@
     key_grad = own_k.reshape(row_count, column_count).astype(jnp.bfloat16)
     value_grad = own_v.reshape(row_count, column_count).astype(jnp.bfloat16)
     attn_dq = grad_q.reshape(row_count, column_count).astype(jnp.bfloat16)
-    row_piece = lax.all_gather(w_kv, "seq", axis=0, tiled=True)
+    ways, here, step = (lax.axis_size("seq"), lax.axis_index("seq"), w_kv.shape[0])
+    shape = [n * ways if d == 0 else n for d, n in enumerate(w_kv.shape)]
+    full = lax.dynamic_update_slice_in_dim(jnp.zeros(shape, w_kv.dtype), w_kv, here * step, axis=0)
+    going_up = going_down = w_kv
+    for far in range(1, ways // 2 + 1):
+        going_up = lax.ppermute(going_up, "seq", [(d, (d + 1) % ways) for d in range(ways)])
+        full = lax.dynamic_update_slice_in_dim(full, going_up, (here - far) % ways * step, axis=0)
+        if 2 * far < ways:
+            going_down = lax.ppermute(going_down, "seq", [(d, (d - 1) % ways) for d in range(ways)])
+            full = lax.dynamic_update_slice_in_dim(
+                full, going_down, (here + far) % ways * step, axis=0
+            )
+    row_piece = full
     from_keys = lax.dot_general(
         row_piece[:, 0, :], key_grad, (((1,), (1,)), ((), ())), preferred_element_type=jnp.float32
     )

time: 313 us -> 346 us (1.11)
  blocking collectives: 54.2 us -> 0 us
  waiting for transfers between devices: 112 us -> 163 us
  starting transfers between devices: 70.6 us -> 97.6 us
  other arithmetic: 7.44 us -> 12 us
    all_gather x1 -> x0, blocking collectives: 54.2 us -> none  [per_device(): row_piece = lax.all_gather(w_kv, 'seq', axis=0, tiled=True)]
    ppermute x0 -> x15, waiting for transfers between devices: none -> 39.2 us  [the longest x8 32.5 us: per_device(): lax.ppermute(going_up, 'seq', [(d, (d + 1) % ways) for d in range(ways)])]
    ppermute x0 -> x15, starting transfers between devices: none -> 31.7 us  [the longest x7 26 us: per_device(): lax.ppermute(going_down, 'seq', [(d, (d - 1) % ways) for d in range(ways)])]
    ppermute x39, waiting for transfers between devices: 112 us -> 122 us  [from_behind(): return lax.ppermute(block, axis, route)]
    ppermute x39, starting transfers between devices: 70.6 us -> 65.9 us  [from_behind(): return lax.ppermute(block, axis, route)]
    dynamic_update_slice x0 -> x15, local copies, waits for them, and re-layouts: none -> 4.63 us  [the longest x7 2.31 us: per_device(): lax.dynamic_update_slice_in_dim(full, going_down, (here + far) % ways * s...]
    unnamed x98 -> x157, local copies, waits for them, and re-layouts: 11.8 us -> 10.3 us
  transfers between devices with their start and end apart: 40 -> 55, of which waited for: 17 -> 29; matrix products, arithmetic and copies ran while one was open for 16% -> 17% of each run, Pallas kernels for 0% -> 0%
where the time goes in v1:
time: 346 us; the launch traced here: 344 us
  waiting for transfers between devices  163 us (47%)
  starting transfers between devices  97.6 us (28%)
  matrix products  34.4 us (10%)
  local copies, waits for them, and re-layouts  20 us (6%)
  between operations  16 us (5%)
  other arithmetic  12 us (3%)
    ppermute x39, waiting for transfers between devices, from_behind(): return lax.ppermute(block, axis, route)  122 us
    ppermute x39, starting transfers between devices, from_behind(): return lax.ppermute(block, axis, route)  65.9 us
    ppermute x8, waiting for transfers between devices, per_device(): lax.ppermute(going_up, 'seq', [(d, (d + 1) % ways) for d in range(ways)])  32.5 us
    ppermute x7, starting transfers between devices, per_device(): lax.ppermute(going_down, 'seq', [(d, (d - 1) % ways) for d in range(ways)])  26 us
    dot_general x53, matrix products, matmul(): return jnp.dot(left_side, right_side, precision=HIGH)  23.5 us
    unnamed x157, local copies, waits for them, and re-layouts  10.3 us
  transfers between devices with their start and end apart: 55, of which 29 were waited for; matrix products, arithmetic and copies ran while one was open for 17% of the time, Pallas kernels for 0%

profile of v1, /device:TPU:0, one launch (start us, length us, event | category | flops | bytes accessed | tf_op | source)
XLA Modules:
  0.0 343.7 jit_solution(11903863473928804057)
XLA Ops:
  7.3 1.4 fusion.202
  8.7 3.0 collective-permute-start.9
  11.7 4.0 %collective-permute-start.10 = (bf16[32,2,256]{2,0,1:T(8,128)(2,1)}, bf16[32,2,256]{2,0,1:T(8,128)(2,1)}, u32[]{:S(2)}, u32[]{:S(2)}) collective-permute-start(bf16[32,2,256]{2,0,1:T(8,128)(2,1)} %get-tuple-element.336), channel_id=1, source_target_pairs={{0,30},{2,0},{4,2},{6,4},{8,6},{10,8},{12,10},{14,12},{16,14},{18,... | collective-permute-start | bytes 98312 | tf_op jit(solution)/shard_map/ppermute | solution.py:193
  30.9 1.9 fusion.49
  37.0 132.2 %while.43 = (s32[]{:T(128)}, f32[2,128,128]{2,1,0:T(8,128)S(1)}, f32[2,128,128]{2,1,0:T(8,128)S(1)}, f32[2,128,128]{2,1,0:T(8,128)S(1)}, s32[]{:T(128)}) while((s32[]{:T(128)}, f32[2,128,128]{2,1,0:T(8,128)S(1)}, f32[2,128,128]{2,1,0:T(8,128)S(1)}, f32[2,128,128]{2,1,0:T(8,128)S(1)}, s32[]{:T(128)}) %tuple.117), condition=%wide.region_9.10_spmd, body=%wide.region_8.9_spmd.sunk | while | flops 50364416 | bytes 1048677 | solution.py:245
  38.6 6.2 %collective-permute-done = f32[2,128,128]{2,1,0:T(8,128)S(1)} collective-permute-done((f32[2,128,128]{2,1,0:T(8,128)S(1)}, f32[2,128,128]{2,1,0:T(8,128)S(1)}, u32[]{:S(2)}, u32[]{:S(2)}) %collective-permute-start) | collective-permute-done | bytes 131104 | tf_op jit(solution)/shard_map/while/body/eval_jaxpr/ppermute | solution.py:14
  46.3 6.5 %collective-permute-done = f32[2,128,128]{2,1,0:T(8,128)S(1)} collective-permute-done((f32[2,128,128]{2,1,0:T(8,128)S(1)}, f32[2,128,128]{2,1,0:T(8,128)S(1)}, u32[]{:S(2)}, u32[]{:S(2)}) %collective-permute-start) | collective-permute-done | bytes 131104 | tf_op jit(solution)/shard_map/while/body/eval_jaxpr/ppermute | solution.py:14
  54.4 6.5 %collective-permute-done = f32[2,128,128]{2,1,0:T(8,128)S(1)} collective-permute-done((f32[2,128,128]{2,1,0:T(8,128)S(1)}, f32[2,128,128]{2,1,0:T(8,128)S(1)}, u32[]{:S(2)}, u32[]{:S(2)}) %collective-permute-start) | collective-permute-done | bytes 131104 | tf_op jit(solution)/shard_map/while/body/eval_jaxpr/ppermute | solution.py:14
  62.4 6.5 %collective-permute-done = f32[2,128,128]{2,1,0:T(8,128)S(1)} collective-permute-done((f32[2,128,128]{2,1,0:T(8,128)S(1)}, f32[2,128,128]{2,1,0:T(8,128)S(1)}, u32[]{:S(2)}, u32[]{:S(2)}) %collective-permute-start) | collective-permute-done | bytes 131104 | tf_op jit(solution)/shard_map/while/body/eval_jaxpr/ppermute | solution.py:14
  70.4 6.5 %collective-permute-done = f32[2,128,128]{2,1,0:T(8,128)S(1)} collective-permute-done((f32[2,128,128]{2,1,0:T(8,128)S(1)}, f32[2,128,128]{2,1,0:T(8,128)S(1)}, u32[]{:S(2)}, u32[]{:S(2)}) %collective-permute-start) | collective-permute-done | bytes 131104 | tf_op jit(solution)/shard_map/while/body/eval_jaxpr/ppermute | solution.py:14
  78.5 7.9 %collective-permute-done = f32[2,128,128]{2,1,0:T(8,128)S(1)} collective-permute-done((f32[2,128,128]{2,1,0:T(8,128)S(1)}, f32[2,128,128]{2,1,0:T(8,128)S(1)}, u32[]{:S(2)}, u32[]{:S(2)}) %collective-permute-start) | collective-permute-done | bytes 131104 | tf_op jit(solution)/shard_map/while/body/eval_jaxpr/ppermute | solution.py:14
  88.0 8.8 %collective-permute-done = f32[2,128,128]{2,1,0:T(8,128)S(1)} collective-permute-done((f32[2,128,128]{2,1,0:T(8,128)S(1)}, f32[2,128,128]{2,1,0:T(8,128)S(1)}, u32[]{:S(2)}, u32[]{:S(2)}) %collective-permute-start) | collective-permute-done | bytes 131104 | tf_op jit(solution)/shard_map/while/body/eval_jaxpr/ppermute | solution.py:14
  98.4 7.9 %collective-permute-done = f32[2,128,128]{2,1,0:T(8,128)S(1)} collective-permute-done((f32[2,128,128]{2,1,0:T(8,128)S(1)}, f32[2,128,128]{2,1,0:T(8,128)S(1)}, u32[]{:S(2)}, u32[]{:S(2)}) %collective-permute-start) | collective-permute-done | bytes 131104 | tf_op jit(solution)/shard_map/while/body/eval_jaxpr/ppermute | solution.py:14
  107.8 7.5 %collective-permute-done = f32[2,128,128]{2,1,0:T(8,128)S(1)} collective-permute-done((f32[2,128,128]{2,1,0:T(8,128)S(1)}, f32[2,128,128]{2,1,0:T(8,128)S(1)}, u32[]{:S(2)}, u32[]{:S(2)}) %collective-permute-start) | collective-permute-done | bytes 131104 | tf_op jit(solution)/shard_map/while/body/eval_jaxpr/ppermute | solution.py:14
  116.9 6.8 %collective-permute-done = f32[2,128,128]{2,1,0:T(8,128)S(1)} collective-permute-done((f32[2,128,128]{2,1,0:T(8,128)S(1)}, f32[2,128,128]{2,1,0:T(8,128)S(1)}, u32[]{:S(2)}, u32[]{:S(2)}) %collective-permute-start) | collective-permute-done | bytes 131104 | tf_op jit(solution)/shard_map/while/body/eval_jaxpr/ppermute | solution.py:14
  125.3 7.4 %collective-permute-done = f32[2,128,128]{2,1,0:T(8,128)S(1)} collective-permute-done((f32[2,128,128]{2,1,0:T(8,128)S(1)}, f32[2,128,128]{2,1,0:T(8,128)S(1)}, u32[]{:S(2)}, u32[]{:S(2)}) %collective-permute-start) | collective-permute-done | bytes 131104 | tf_op jit(solution)/shard_map/while/body/eval_jaxpr/ppermute | solution.py:14
  134.2 7.4 %collective-permute-done = f32[2,128,128]{2,1,0:T(8,128)S(1)} collective-permute-done((f32[2,128,128]{2,1,0:T(8,128)S(1)}, f32[2,128,128]{2,1,0:T(8,128)S(1)}, u32[]{:S(2)}, u32[]{:S(2)}) %collective-permute-start) | collective-permute-done | bytes 131104 | tf_op jit(solution)/shard_map/while/body/eval_jaxpr/ppermute | solution.py:14
  143.2 7.6 %collective-permute-done = f32[2,128,128]{2,1,0:T(8,128)S(1)} collective-permute-done((f32[2,128,128]{2,1,0:T(8,128)S(1)}, f32[2,128,128]{2,1,0:T(8,128)S(1)}, u32[]{:S(2)}, u32[]{:S(2)}) %collective-permute-start) | collective-permute-done | bytes 131104 | tf_op jit(solution)/shard_map/while/body/eval_jaxpr/ppermute | solution.py:14
  152.3 7.6 %collective-permute-done = f32[2,128,128]{2,1,0:T(8,128)S(1)} collective-permute-done((f32[2,128,128]{2,1,0:T(8,128)S(1)}, f32[2,128,128]{2,1,0:T(8,128)S(1)}, u32[]{:S(2)}, u32[]{:S(2)}) %collective-permute-start) | collective-permute-done | bytes 131104 | tf_op jit(solution)/shard_map/while/body/eval_jaxpr/ppermute | solution.py:14
  161.6 7.6 %collective-permute-done = f32[2,128,128]{2,1,0:T(8,128)S(1)} collective-permute-done((f32[2,128,128]{2,1,0:T(8,128)S(1)}, f32[2,128,128]{2,1,0:T(8,128)S(1)}, u32[]{:S(2)}, u32[]{:S(2)}) %collective-permute-start) | collective-permute-done | bytes 131104 | tf_op jit(solution)/shard_map/while/body/eval_jaxpr/ppermute | solution.py:14
  169.2 1.5 collective-permute-start.34
  191.6 1.5 fusion.40
  204.1 5.3 %collective-permute-done.35 = f32[2,2,128]{2,1,0:T(2,128)S(1)} collective-permute-done((f32[2,2,128]{2,1,0:T(2,128)}, f32[2,2,128]{2,1,0:T(2,128)S(1)}, u32[]{:S(2)}, u32[]{:S(2)}) %collective-permute-start.35) | collective-permute-done | bytes 2080 | tf_op jit(solution)/shard_map/ppermute | solution.py:14
  210.7 3.2 collective-permute-done.36
  215.2 3.6 %collective-permute-done.37 = f32[2,2,128]{2,1,0:T(2,128)S(1)} collective-permute-done((f32[2,2,128]{2,1,0:T(2,128)}, f32[2,2,128]{2,1,0:T(2,128)S(1)}, u32[]{:S(2)}, u32[]{:S(2)}) %collective-permute-start.37) | collective-permute-done | bytes 2080 | tf_op jit(solution)/shard_map/ppermute | solution.py:14
  226.4 1.5 collective-permute-start.11
  228.7 13.1 %collective-permute-done.11 = bf16[32,2,256]{2,0,1:T(8,128)(2,1)S(1)} collective-permute-done((bf16[32,2,256]{2,0,1:T(8,128)(2,1)}, bf16[32,2,256]{2,0,1:T(8,128)(2,1)S(1)}, u32[]{:S(2)}, u32[]{:S(2)}) %collective-permute-start.11) | collective-permute-done | bytes 32800 | tf_op jit(solution)/shard_map/ppermute | solution.py:190
  242.1 3.8 %collective-permute-done.12 = bf16[32,2,256]{2,0,1:T(8,128)(2,1)S(1)} collective-permute-done((bf16[32,2,256]{2,0,1:T(8,128)(2,1)}, bf16[32,2,256]{2,0,1:T(8,128)(2,1)S(1)}, u32[]{:S(2)}, u32[]{:S(2)}) %collective-permute-start.12) | collective-permute-done | bytes 32800 | tf_op jit(solution)/shard_map/ppermute | solution.py:193
  245.9 7.6 %collective-permute-done.13 = bf16[32,2,256]{2,0,1:T(8,128)(2,1)} collective-permute-done((bf16[32,2,256]{2,0,1:T(8,128)(2,1)S(1)}, bf16[32,2,256]{2,0,1:T(8,128)(2,1)}, u32[]{:S(2)}, u32[]{:S(2)}) %collective-permute-start.13) | collective-permute-done | bytes 32800 | tf_op jit(solution)/shard_map/ppermute | solution.py:190
  254.6 2.9 collective-permute-done.14
  263.7 5.5 %collective-permute-start.1 = (bf16[2,128,256]{1,2,0:T(8,128)(2,1)}, bf16[2,128,256]{1,2,0:T(8,128)(2,1)S(1)}, u32[]{:S(2)}, u32[]{:S(2)}) collective-permute-start(bf16[2,128,256]{1,2,0:T(8,128)(2,1)} %pad_maximum_fusion), channel_id=1, source_target_pairs={{0,16},{2,18},{4,20},{6,22},{8,24},{10,26},{12,28},{14,30},{1,17},... | collective-permute-start | bytes 393224 | tf_op jit(solution)/shard_map/ppermute | solution.py:14
  269.2 6.4 %collective-permute-start.2 = (bf16[2,128,256]{1,2,0:T(8,128)(2,1)}, bf16[2,128,256]{1,2,0:T(8,128)(2,1)S(1)}, u32[]{:S(2)}, u32[]{:S(2)}) collective-permute-start(bf16[2,128,256]{1,2,0:T(8,128)(2,1)} %pad_maximum_fusion), channel_id=1, source_target_pairs={{0,14},{2,16},{4,18},{6,20},{8,22},{10,24},{12,26},{14,28},{16,30}... | collective-permute-start | bytes 393224 | tf_op jit(solution)/shard_map/ppermute | solution.py:14
  275.6 2.2 collective-permute-start.3
  277.9 1.3 collective-permute-start.4
  279.2 1.6 collective-permute-start.5
  281.0 3.9 %collective-permute-start.6 = (bf16[2,128,256]{1,2,0:T(8,128)(2,1)}, bf16[2,128,256]{1,2,0:T(8,128)(2,1)S(1)}, u32[]{:S(2)}, u32[]{:S(2)}) collective-permute-start(bf16[2,128,256]{1,2,0:T(8,128)(2,1)} %pad_maximum_fusion), channel_id=1, source_target_pairs={{0,6},{2,8},{4,10},{6,12},{8,14},{10,16},{12,18},{14,20},{16,22},{... | collective-permute-start | bytes 393224 | tf_op jit(solution)/shard_map/ppermute | solution.py:14
  284.9 1.6 collective-permute-start.7
  286.5 3.5 %collective-permute-start.8 = (bf16[2,128,256]{1,2,0:T(8,128)(2,1)}, bf16[2,128,256]{1,2,0:T(8,128)(2,1)S(1)}, u32[]{:S(2)}, u32[]{:S(2)}) collective-permute-start(bf16[2,128,256]{1,2,0:T(8,128)(2,1)} %pad_maximum_fusion), channel_id=1, source_target_pairs={{0,2},{2,4},{4,6},{6,8},{8,10},{10,12},{12,14},{14,16},{16,18},{18... | collective-permute-start | bytes 393224 | tf_op jit(solution)/shard_map/ppermute | solution.py:14
  291.3 4.5 %collective-permute-start.16 = (bf16[32,2,256]{2,0,1:T(8,128)(2,1)}, bf16[32,2,256]{2,0,1:T(8,128)(2,1)}, u32[]{:S(2)}, u32[]{:S(2)}) collective-permute-start(bf16[32,2,256]{2,0,1:T(8,128)(2,1)} %collective-permute-done.14), channel_id=1, source_target_pairs={{0,30},{2,0},{4,2},{6,4},{8,6},{10,8},{12,10},{14,12},{16,14},{18,... | collective-permute-start | bytes 98312 | tf_op jit(solution)/shard_map/ppermute | solution.py:193
  297.5 2.2 fusion.33
  300.2 5.6 %collective-permute-start.18 = (bf16[32,2,256]{2,0,1:T(8,128)(2,1)}, bf16[32,2,256]{2,0,1:T(8,128)(2,1)S(1)}, u32[]{:S(2)}, u32[]{:S(2)}) collective-permute-start(bf16[32,2,256]{2,0,1:T(8,128)(2,1)} %collective-permute-done.16), channel_id=1, source_target_pairs={{0,30},{2,0},{4,2},{6,4},{8,6},{10,8},{12,10},{14,12},{16,14},{18,... | collective-permute-start | bytes 98312 | tf_op jit(solution)/shard_map/ppermute | solution.py:193
  307.9 5.6 %collective-permute-start.20 = (bf16[32,2,256]{2,0,1:T(8,128)(2,1)S(1)}, bf16[32,2,256]{2,0,1:T(8,128)(2,1)S(1)}, u32[]{:S(2)}, u32[]{:S(2)}) collective-permute-start(bf16[32,2,256]{2,0,1:T(8,128)(2,1)S(1)} %collective-permute-done.18), channel_id=1, source_target_pairs={{0,30},{2,0},{4,2},{6,4},{8,6},{10,8},{12,10},{14,12},{16,14},{18,... | collective-permute-start | bytes 98312 | tf_op jit(solution)/shard_map/ppermute | solution.py:193
  313.5 1.9 collective-permute-done.19
  315.4 5.6 %collective-permute-start.22 = (bf16[32,2,256]{2,0,1:T(8,128)(2,1)S(1)}, bf16[32,2,256]{2,0,1:T(8,128)(2,1)S(1)}, u32[]{:S(2)}, u32[]{:S(2)}) collective-permute-start(bf16[32,2,256]{2,0,1:T(8,128)(2,1)S(1)} %collective-permute-done.20), channel_id=1, source_target_pairs={{0,30},{2,0},{4,2},{6,4},{8,6},{10,8},{12,10},{14,12},{16,14},{18,... | collective-permute-start | bytes 98312 | tf_op jit(solution)/shard_map/ppermute | solution.py:193
  321.0 1.9 collective-permute-done.21
  322.9 7.5 %collective-permute-done.23 = bf16[32,2,256]{2,0,1:T(8,128)(2,1)S(1)} collective-permute-done((bf16[32,2,256]{2,0,1:T(8,128)(2,1)S(1)}, bf16[32,2,256]{2,0,1:T(8,128)(2,1)S(1)}, u32[]{:S(2)}, u32[]{:S(2)}) %collective-permute-start.23) | collective-permute-done | bytes 32800 | tf_op jit(solution)/shard_map/ppermute | solution.py:190
  333.8 1.6 reduce-scatter.2.cloned.1.call-done
  335.4 1.5 convert_element_type.147
  (395 shorter events, 102.8 us)
Async XLA Ops:
  7.2 328.1 %reduce-scatter.2.cloned.1.call-start = ((), (), s32[]{:S(2)}) async-start(), calls=%async_computation.1 | async-start | bytes 393216 | tf_op jit(solution)/shard_map/reduce_scatter | solution.py:204
  8.7 215.7 %collective-permute-start.9 = (bf16[32,2,256]{2,0,1:T(8,128)(2,1)}, bf16[32,2,256]{2,0,1:T(8,128)(2,1)}, u32[]{:S(2)}, u32[]{:S(2)}) collective-permute-start(bf16[32,2,256]{2,0,1:T(8,128)(2,1)} %get-tuple-element.336), channel_id=1, source_target_pairs={{0,2},{2,4},{4,6},{6,8},{8,10},{10,12},{12,14},{14,16},{16,18},{18... | collective-permute-start | bytes 98312 | tf_op jit(solution)/shard_map/ppermute | solution.py:190
  11.7 214.8 %collective-permute-start.10 = (bf16[32,2,256]{2,0,1:T(8,128)(2,1)}, bf16[32,2,256]{2,0,1:T(8,128)(2,1)}, u32[]{:S(2)}, u32[]{:S(2)}) collective-permute-start(bf16[32,2,256]{2,0,1:T(8,128)(2,1)} %get-tuple-element.336), channel_id=1, source_target_pairs={{0,30},{2,0},{4,2},{6,4},{8,6},{10,8},{12,10},{14,12},{16,14},{18,... | collective-permute-start | bytes 98312 | tf_op jit(solution)/shard_map/ppermute | solution.py:193
  18.3 179.9 %collective-permute-start.32 = (f32[2,2,128]{2,1,0:T(2,128)}, f32[2,2,128]{2,1,0:T(2,128)}, u32[]{:S(2)}, u32[]{:S(2)}) collective-permute-start(f32[2,2,128]{2,1,0:T(2,128)} %get-tuple-element.352), channel_id=1, source_target_pairs={{2,0},{4,2},{6,4},{8,6},{10,8},{12,10},{14,12},{16,14},{18,16},{20... | collective-permute-start | bytes 6152 | tf_op jit(solution)/shard_map/ppermute | solution.py:14
  19.6 180.6 %collective-permute-start.33 = (f32[2,2,128]{2,1,0:T(2,128)}, f32[2,2,128]{2,1,0:T(2,128)}, u32[]{:S(2)}, u32[]{:S(2)}) collective-permute-start(f32[2,2,128]{2,1,0:T(2,128)} %get-tuple-element.352), channel_id=1, source_target_pairs={{4,0},{6,2},{8,4},{10,6},{12,8},{14,10},{16,12},{18,14},{20,16},{2... | collective-permute-start | bytes 6152 | tf_op jit(solution)/shard_map/ppermute | solution.py:14
  45.0 7.8 %collective-permute-start = (f32[2,128,128]{2,1,0:T(8,128)S(1)}, f32[2,128,128]{2,1,0:T(8,128)S(1)}, u32[]{:S(2)}, u32[]{:S(2)}) collective-permute-start(f32[2,128,128]{2,1,0:T(8,128)S(1)} %convolution_add_fusion.20), channel_id=1, source_target_pairs={{2,0},{4,2},{6,4},{8,6},{10,8},{12,10},{14,12},{16,14},{18,16},{20... | collective-permute-start | bytes 393224 | tf_op jit(solution)/shard_map/while/body/eval_jaxpr/ppermute | solution.py:14
  53.1 7.8 %collective-permute-start = (f32[2,128,128]{2,1,0:T(8,128)S(1)}, f32[2,128,128]{2,1,0:T(8,128)S(1)}, u32[]{:S(2)}, u32[]{:S(2)}) collective-permute-start(f32[2,128,128]{2,1,0:T(8,128)S(1)} %convolution_add_fusion.20), channel_id=1, source_target_pairs={{2,0},{4,2},{6,4},{8,6},{10,8},{12,10},{14,12},{16,14},{18,16},{20... | collective-permute-start | bytes 393224 | tf_op jit(solution)/shard_map/while/body/eval_jaxpr/ppermute | solution.py:14
  61.1 7.8 %collective-permute-start = (f32[2,128,128]{2,1,0:T(8,128)S(1)}, f32[2,128,128]{2,1,0:T(8,128)S(1)}, u32[]{:S(2)}, u32[]{:S(2)}) collective-permute-start(f32[2,128,128]{2,1,0:T(8,128)S(1)} %convolution_add_fusion.20), channel_id=1, source_target_pairs={{2,0},{4,2},{6,4},{8,6},{10,8},{12,10},{14,12},{16,14},{18,16},{20... | collective-permute-start | bytes 393224 | tf_op jit(solution)/shard_map/while/body/eval_jaxpr/ppermute | solution.py:14
  69.1 7.8 %collective-permute-start = (f32[2,128,128]{2,1,0:T(8,128)S(1)}, f32[2,128,128]{2,1,0:T(8,128)S(1)}, u32[]{:S(2)}, u32[]{:S(2)}) collective-permute-start(f32[2,128,128]{2,1,0:T(8,128)S(1)} %convolution_add_fusion.20), channel_id=1, source_target_pairs={{2,0},{4,2},{6,4},{8,6},{10,8},{12,10},{14,12},{16,14},{18,16},{20... | collective-permute-start | bytes 393224 | tf_op jit(solution)/shard_map/while/body/eval_jaxpr/ppermute | solution.py:14
  77.2 9.2 %collective-permute-start = (f32[2,128,128]{2,1,0:T(8,128)S(1)}, f32[2,128,128]{2,1,0:T(8,128)S(1)}, u32[]{:S(2)}, u32[]{:S(2)}) collective-permute-start(f32[2,128,128]{2,1,0:T(8,128)S(1)} %convolution_add_fusion.20), channel_id=1, source_target_pairs={{2,0},{4,2},{6,4},{8,6},{10,8},{12,10},{14,12},{16,14},{18,16},{20... | collective-permute-start | bytes 393224 | tf_op jit(solution)/shard_map/while/body/eval_jaxpr/ppermute | solution.py:14
  86.7 10.1 %collective-permute-start = (f32[2,128,128]{2,1,0:T(8,128)S(1)}, f32[2,128,128]{2,1,0:T(8,128)S(1)}, u32[]{:S(2)}, u32[]{:S(2)}) collective-permute-start(f32[2,128,128]{2,1,0:T(8,128)S(1)} %convolution_add_fusion.20), channel_id=1, source_target_pairs={{2,0},{4,2},{6,4},{8,6},{10,8},{12,10},{14,12},{16,14},{18,16},{20... | collective-permute-start | bytes 393224 | tf_op jit(solution)/shard_map/while/body/eval_jaxpr/ppermute | solution.py:14
  97.1 9.2 %collective-permute-start = (f32[2,128,128]{2,1,0:T(8,128)S(1)}, f32[2,128,128]{2,1,0:T(8,128)S(1)}, u32[]{:S(2)}, u32[]{:S(2)}) collective-permute-start(f32[2,128,128]{2,1,0:T(8,128)S(1)} %convolution_add_fusion.20), channel_id=1, source_target_pairs={{2,0},{4,2},{6,4},{8,6},{10,8},{12,10},{14,12},{16,14},{18,16},{20... | collective-permute-start | bytes 393224 | tf_op jit(solution)/shard_map/while/body/eval_jaxpr/ppermute | solution.py:14
  106.5 8.8 %collective-permute-start = (f32[2,128,128]{2,1,0:T(8,128)S(1)}, f32[2,128,128]{2,1,0:T(8,128)S(1)}, u32[]{:S(2)}, u32[]{:S(2)}) collective-permute-start(f32[2,128,128]{2,1,0:T(8,128)S(1)} %convolution_add_fusion.20), channel_id=1, source_target_pairs={{2,0},{4,2},{6,4},{8,6},{10,8},{12,10},{14,12},{16,14},{18,16},{20... | collective-permute-start | bytes 393224 | tf_op jit(solution)/shard_map/while/body/eval_jaxpr/ppermute | solution.py:14
  115.6 8.1 %collective-permute-start = (f32[2,128,128]{2,1,0:T(8,128)S(1)}, f32[2,128,128]{2,1,0:T(8,128)S(1)}, u32[]{:S(2)}, u32[]{:S(2)}) collective-permute-start(f32[2,128,128]{2,1,0:T(8,128)S(1)} %convolution_add_fusion.20), channel_id=1, source_target_pairs={{2,0},{4,2},{6,4},{8,6},{10,8},{12,10},{14,12},{16,14},{18,16},{20... | collective-permute-start | bytes 393224 | tf_op jit(solution)/shard_map/while/body/eval_jaxpr/ppermute | solution.py:14
  124.0 8.7 %collective-permute-start = (f32[2,128,128]{2,1,0:T(8,128)S(1)}, f32[2,128,128]{2,1,0:T(8,128)S(1)}, u32[]{:S(2)}, u32[]{:S(2)}) collective-permute-start(f32[2,128,128]{2,1,0:T(8,128)S(1)} %convolution_add_fusion.20), channel_id=1, source_target_pairs={{2,0},{4,2},{6,4},{8,6},{10,8},{12,10},{14,12},{16,14},{18,16},{20... | collective-permute-start | bytes 393224 | tf_op jit(solution)/shard_map/while/body/eval_jaxpr/ppermute | solution.py:14
  132.9 8.7 %collective-permute-start = (f32[2,128,128]{2,1,0:T(8,128)S(1)}, f32[2,128,128]{2,1,0:T(8,128)S(1)}, u32[]{:S(2)}, u32[]{:S(2)}) collective-permute-start(f32[2,128,128]{2,1,0:T(8,128)S(1)} %convolution_add_fusion.20), channel_id=1, source_target_pairs={{2,0},{4,2},{6,4},{8,6},{10,8},{12,10},{14,12},{16,14},{18,16},{20... | collective-permute-start | bytes 393224 | tf_op jit(solution)/shard_map/while/body/eval_jaxpr/ppermute | solution.py:14
  141.9 8.9 %collective-permute-start = (f32[2,128,128]{2,1,0:T(8,128)S(1)}, f32[2,128,128]{2,1,0:T(8,128)S(1)}, u32[]{:S(2)}, u32[]{:S(2)}) collective-permute-start(f32[2,128,128]{2,1,0:T(8,128)S(1)} %convolution_add_fusion.20), channel_id=1, source_target_pairs={{2,0},{4,2},{6,4},{8,6},{10,8},{12,10},{14,12},{16,14},{18,16},{20... | collective-permute-start | bytes 393224 | tf_op jit(solution)/shard_map/while/body/eval_jaxpr/ppermute | solution.py:14
  151.0 8.9 %collective-permute-start = (f32[2,128,128]{2,1,0:T(8,128)S(1)}, f32[2,128,128]{2,1,0:T(8,128)S(1)}, u32[]{:S(2)}, u32[]{:S(2)}) collective-permute-start(f32[2,128,128]{2,1,0:T(8,128)S(1)} %convolution_add_fusion.20), channel_id=1, source_target_pairs={{2,0},{4,2},{6,4},{8,6},{10,8},{12,10},{14,12},{16,14},{18,16},{20... | collective-permute-start | bytes 393224 | tf_op jit(solution)/shard_map/while/body/eval_jaxpr/ppermute | solution.py:14
  160.2 8.9 %collective-permute-start = (f32[2,128,128]{2,1,0:T(8,128)S(1)}, f32[2,128,128]{2,1,0:T(8,128)S(1)}, u32[]{:S(2)}, u32[]{:S(2)}) collective-permute-start(f32[2,128,128]{2,1,0:T(8,128)S(1)} %convolution_add_fusion.20), channel_id=1, source_target_pairs={{2,0},{4,2},{6,4},{8,6},{10,8},{12,10},{14,12},{16,14},{18,16},{20... | collective-permute-start | bytes 393224 | tf_op jit(solution)/shard_map/while/body/eval_jaxpr/ppermute | solution.py:14
  169.2 33.0 %collective-permute-start.34 = (f32[2,2,128]{2,1,0:T(2,128)}, f32[2,2,128]{2,1,0:T(2,128)}, u32[]{:S(2)}, u32[]{:S(2)}) collective-permute-start(f32[2,2,128]{2,1,0:T(2,128)} %get-tuple-element.352), channel_id=1, source_target_pairs={{6,0},{8,2},{10,4},{12,6},{14,8},{16,10},{18,12},{20,14},{22,16},{... | collective-permute-start | bytes 6152 | tf_op jit(solution)/shard_map/ppermute | solution.py:14
  198.2 11.2 %collective-permute-start.35 = (f32[2,2,128]{2,1,0:T(2,128)}, f32[2,2,128]{2,1,0:T(2,128)S(1)}, u32[]{:S(2)}, u32[]{:S(2)}) collective-permute-start(f32[2,2,128]{2,1,0:T(2,128)} %get-tuple-element.352), channel_id=1, source_target_pairs={{8,0},{10,2},{12,4},{14,6},{16,8},{18,10},{20,12},{22,14},{24,16},... | collective-permute-start | bytes 6152 | tf_op jit(solution)/shard_map/ppermute | solution.py:14
  200.2 13.7 %collective-permute-start.36 = (f32[2,2,128]{2,1,0:T(2,128)}, f32[2,2,128]{2,1,0:T(2,128)S(1)}, u32[]{:S(2)}, u32[]{:S(2)}) collective-permute-start(f32[2,2,128]{2,1,0:T(2,128)} %get-tuple-element.352), channel_id=1, source_target_pairs={{10,0},{12,2},{14,4},{16,6},{18,8},{20,10},{22,12},{24,14},{26,16}... | collective-permute-start | bytes 6152 | tf_op jit(solution)/shard_map/ppermute | solution.py:14
  202.2 16.7 %collective-permute-start.37 = (f32[2,2,128]{2,1,0:T(2,128)}, f32[2,2,128]{2,1,0:T(2,128)S(1)}, u32[]{:S(2)}, u32[]{:S(2)}) collective-permute-start(f32[2,2,128]{2,1,0:T(2,128)} %get-tuple-element.352), channel_id=1, source_target_pairs={{12,0},{14,2},{16,4},{18,6},{20,8},{22,10},{24,12},{26,14},{28,16}... | collective-permute-start | bytes 6152 | tf_op jit(solution)/shard_map/ppermute | solution.py:14
  209.4 12.0 %collective-permute-start.38 = (f32[2,2,128]{2,1,0:T(2,128)}, f32[2,2,128]{2,1,0:T(2,128)S(1)}, u32[]{:S(2)}, u32[]{:S(2)}) collective-permute-start(f32[2,2,128]{2,1,0:T(2,128)} %get-tuple-element.352), channel_id=1, source_target_pairs={{14,0},{16,2},{18,4},{20,6},{22,8},{24,10},{26,12},{28,14},{30,16}... | collective-permute-start | bytes 6152 | tf_op jit(solution)/shard_map/ppermute | solution.py:14
  213.9 9.1 %collective-permute-start.39 = (f32[2,2,128]{2,1,0:T(2,128)}, f32[2,2,128]{2,1,0:T(2,128)S(1)}, u32[]{:S(2)}, u32[]{:S(2)}) collective-permute-start(f32[2,2,128]{2,1,0:T(2,128)} %get-tuple-element.352), channel_id=1, source_target_pairs={{16,0},{18,2},{20,4},{22,6},{24,8},{26,10},{28,12},{30,14},{17,1},... | collective-permute-start | bytes 6152 | tf_op jit(solution)/shard_map/ppermute | solution.py:14
  218.9 40.7 %collective-permute-start.24 = (bf16[2,128,256]{1,2,0:T(8,128)(2,1)S(1)}, bf16[2,128,256]{1,2,0:T(8,128)(2,1)S(1)}, u32[]{:S(2)}, u32[]{:S(2)}) collective-permute-start(bf16[2,128,256]{1,2,0:T(8,128)(2,1)S(1)} %get-tuple-element.334), channel_id=1, source_target_pairs={{2,0},{4,2},{6,4},{8,6},{10,8},{12,10},{14,12},{16,14},{18,16},{20... | collective-permute-start | bytes 393224 | tf_op jit(solution)/shard_map/ppermute | solution.py:14
  221.4 39.5 %collective-permute-start.25 = (bf16[2,128,256]{1,2,0:T(8,128)(2,1)S(1)}, bf16[2,128,256]{1,2,0:T(8,128)(2,1)S(1)}, u32[]{:S(2)}, u32[]{:S(2)}) collective-permute-start(bf16[2,128,256]{1,2,0:T(8,128)(2,1)S(1)} %get-tuple-element.334), channel_id=1, source_target_pairs={{4,0},{6,2},{8,4},{10,6},{12,8},{14,10},{16,12},{18,14},{20,16},{2... | collective-permute-start | bytes 393224 | tf_op jit(solution)/shard_map/ppermute | solution.py:14
  223.0 39.3 %collective-permute-start.26 = (bf16[2,128,256]{1,2,0:T(8,128)(2,1)S(1)}, bf16[2,128,256]{1,2,0:T(8,128)(2,1)S(1)}, u32[]{:S(2)}, u32[]{:S(2)}) collective-permute-start(bf16[2,128,256]{1,2,0:T(8,128)(2,1)S(1)} %get-tuple-element.334), channel_id=1, source_target_pairs={{6,0},{8,2},{10,4},{12,6},{14,8},{16,10},{18,12},{20,14},{22,16},{... | collective-permute-start | bytes 393224 | tf_op jit(solution)/shard_map/ppermute | solution.py:14
  224.4 39.3 %collective-permute-start.27 = (bf16[2,128,256]{1,2,0:T(8,128)(2,1)S(1)}, bf16[2,128,256]{1,2,0:T(8,128)(2,1)S(1)}, u32[]{:S(2)}, u32[]{:S(2)}) collective-permute-start(bf16[2,128,256]{1,2,0:T(8,128)(2,1)S(1)} %get-tuple-element.334), channel_id=1, source_target_pairs={{8,0},{10,2},{12,4},{14,6},{16,8},{18,10},{20,12},{22,14},{24,16},... | collective-permute-start | bytes 393224 | tf_op jit(solution)/shard_map/ppermute | solution.py:14
  226.4 15.4 %collective-permute-start.11 = (bf16[32,2,256]{2,0,1:T(8,128)(2,1)}, bf16[32,2,256]{2,0,1:T(8,128)(2,1)S(1)}, u32[]{:S(2)}, u32[]{:S(2)}) collective-permute-start(bf16[32,2,256]{2,0,1:T(8,128)(2,1)} %collective-permute-done.9), channel_id=1, source_target_pairs={{0,2},{2,4},{4,6},{6,8},{8,10},{10,12},{12,14},{14,16},{16,18},{18... | collective-permute-start | bytes 98312 | tf_op jit(solution)/shard_map/ppermute | solution.py:190
  245.9 7.6 %collective-permute-start.13 = (bf16[32,2,256]{2,0,1:T(8,128)(2,1)S(1)}, bf16[32,2,256]{2,0,1:T(8,128)(2,1)}, u32[]{:S(2)}, u32[]{:S(2)}) collective-permute-start(bf16[32,2,256]{2,0,1:T(8,128)(2,1)S(1)} %collective-permute-done.11), channel_id=1, source_target_pairs={{0,2},{2,4},{4,6},{6,8},{8,10},{10,12},{12,14},{14,16},{16,18},{18... | collective-permute-start | bytes 98312 | tf_op jit(solution)/shard_map/ppermute | solution.py:190
  257.6 11.6 %collective-permute-start.28 = (bf16[2,128,256]{1,2,0:T(8,128)(2,1)S(1)}, bf16[2,128,256]{1,2,0:T(8,128)(2,1)S(1)}, u32[]{:S(2)}, u32[]{:S(2)}) collective-permute-start(bf16[2,128,256]{1,2,0:T(8,128)(2,1)S(1)} %get-tuple-element.334), channel_id=1, source_target_pairs={{10,0},{12,2},{14,4},{16,6},{18,8},{20,10},{22,12},{24,14},{26,16}... | collective-permute-start | bytes 393224 | tf_op jit(solution)/shard_map/ppermute | solution.py:14
  259.6 16.0 %collective-permute-start.29 = (bf16[2,128,256]{1,2,0:T(8,128)(2,1)S(1)}, bf16[2,128,256]{1,2,0:T(8,128)(2,1)S(1)}, u32[]{:S(2)}, u32[]{:S(2)}) collective-permute-start(bf16[2,128,256]{1,2,0:T(8,128)(2,1)S(1)} %get-tuple-element.334), channel_id=1, source_target_pairs={{12,0},{14,2},{16,4},{18,6},{20,8},{22,10},{24,12},{26,14},{28,16}... | collective-permute-start | bytes 393224 | tf_op jit(solution)/shard_map/ppermute | solution.py:14
  261.0 16.9 %collective-permute-start.30 = (bf16[2,128,256]{1,2,0:T(8,128)(2,1)S(1)}, bf16[2,128,256]{1,2,0:T(8,128)(2,1)S(1)}, u32[]{:S(2)}, u32[]{:S(2)}) collective-permute-start(bf16[2,128,256]{1,2,0:T(8,128)(2,1)S(1)} %get-tuple-element.334), channel_id=1, source_target_pairs={{14,0},{16,2},{18,4},{20,6},{22,8},{24,10},{26,12},{28,14},{30,16}... | collective-permute-start | bytes 393224 | tf_op jit(solution)/shard_map/ppermute | solution.py:14
  262.3 16.9 %collective-permute-start.31 = (bf16[2,128,256]{1,2,0:T(8,128)(2,1)S(1)}, bf16[2,128,256]{1,2,0:T(8,128)(2,1)S(1)}, u32[]{:S(2)}, u32[]{:S(2)}) collective-permute-start(bf16[2,128,256]{1,2,0:T(8,128)(2,1)S(1)} %get-tuple-element.334), channel_id=1, source_target_pairs={{16,0},{18,2},{20,4},{22,6},{24,8},{26,10},{28,12},{30,14},{17,1},... | collective-permute-start | bytes 393224 | tf_op jit(solution)/shard_map/ppermute | solution.py:14
  263.7 17.3 %collective-permute-start.1 = (bf16[2,128,256]{1,2,0:T(8,128)(2,1)}, bf16[2,128,256]{1,2,0:T(8,128)(2,1)S(1)}, u32[]{:S(2)}, u32[]{:S(2)}) collective-permute-start(bf16[2,128,256]{1,2,0:T(8,128)(2,1)} %pad_maximum_fusion), channel_id=1, source_target_pairs={{0,16},{2,18},{4,20},{6,22},{8,24},{10,26},{12,28},{14,30},{1,17},... | collective-permute-start | bytes 393224 | tf_op jit(solution)/shard_map/ppermute | solution.py:14
  269.2 15.7 %collective-permute-start.2 = (bf16[2,128,256]{1,2,0:T(8,128)(2,1)}, bf16[2,128,256]{1,2,0:T(8,128)(2,1)S(1)}, u32[]{:S(2)}, u32[]{:S(2)}) collective-permute-start(bf16[2,128,256]{1,2,0:T(8,128)(2,1)} %pad_maximum_fusion), channel_id=1, source_target_pairs={{0,14},{2,16},{4,18},{6,20},{8,22},{10,24},{12,26},{14,28},{16,30}... | collective-permute-start | bytes 393224 | tf_op jit(solution)/shard_map/ppermute | solution.py:14
  275.6 10.9 %collective-permute-start.3 = (bf16[2,128,256]{1,2,0:T(8,128)(2,1)}, bf16[2,128,256]{1,2,0:T(8,128)(2,1)S(1)}, u32[]{:S(2)}, u32[]{:S(2)}) collective-permute-start(bf16[2,128,256]{1,2,0:T(8,128)(2,1)} %pad_maximum_fusion), channel_id=1, source_target_pairs={{0,12},{2,14},{4,16},{6,18},{8,20},{10,22},{12,24},{14,26},{16,28}... | collective-permute-start | bytes 393224 | tf_op jit(solution)/shard_map/ppermute | solution.py:14
  277.9 12.2 %collective-permute-start.4 = (bf16[2,128,256]{1,2,0:T(8,128)(2,1)}, bf16[2,128,256]{1,2,0:T(8,128)(2,1)S(1)}, u32[]{:S(2)}, u32[]{:S(2)}) collective-permute-start(bf16[2,128,256]{1,2,0:T(8,128)(2,1)} %pad_maximum_fusion), channel_id=1, source_target_pairs={{0,10},{2,12},{4,14},{6,16},{8,18},{10,20},{12,22},{14,24},{16,26}... | collective-permute-start | bytes 393224 | tf_op jit(solution)/shard_map/ppermute | solution.py:14
  279.2 12.1 %collective-permute-start.5 = (bf16[2,128,256]{1,2,0:T(8,128)(2,1)}, bf16[2,128,256]{1,2,0:T(8,128)(2,1)S(1)}, u32[]{:S(2)}, u32[]{:S(2)}) collective-permute-start(bf16[2,128,256]{1,2,0:T(8,128)(2,1)} %pad_maximum_fusion), channel_id=1, source_target_pairs={{0,8},{2,10},{4,12},{6,14},{8,16},{10,18},{12,20},{14,22},{16,24},... | collective-permute-start | bytes 393224 | tf_op jit(solution)/shard_map/ppermute | solution.py:14
  281.0 14.9 %collective-permute-start.6 = (bf16[2,128,256]{1,2,0:T(8,128)(2,1)}, bf16[2,128,256]{1,2,0:T(8,128)(2,1)S(1)}, u32[]{:S(2)}, u32[]{:S(2)}) collective-permute-start(bf16[2,128,256]{1,2,0:T(8,128)(2,1)} %pad_maximum_fusion), channel_id=1, source_target_pairs={{0,6},{2,8},{4,10},{6,12},{8,14},{10,16},{12,18},{14,20},{16,22},{... | collective-permute-start | bytes 393224 | tf_op jit(solution)/shard_map/ppermute | solution.py:14
  284.9 11.0 %collective-permute-start.7 = (bf16[2,128,256]{1,2,0:T(8,128)(2,1)}, bf16[2,128,256]{1,2,0:T(8,128)(2,1)S(1)}, u32[]{:S(2)}, u32[]{:S(2)}) collective-permute-start(bf16[2,128,256]{1,2,0:T(8,128)(2,1)} %pad_maximum_fusion), channel_id=1, source_target_pairs={{0,4},{2,6},{4,8},{6,10},{8,12},{10,14},{12,16},{14,18},{16,20},{1... | collective-permute-start | bytes 393224 | tf_op jit(solution)/shard_map/ppermute | solution.py:14
  286.5 9.4 %collective-permute-start.8 = (bf16[2,128,256]{1,2,0:T(8,128)(2,1)}, bf16[2,128,256]{1,2,0:T(8,128)(2,1)S(1)}, u32[]{:S(2)}, u32[]{:S(2)}) collective-permute-start(bf16[2,128,256]{1,2,0:T(8,128)(2,1)} %pad_maximum_fusion), channel_id=1, source_target_pairs={{0,2},{2,4},{4,6},{6,8},{8,10},{10,12},{12,14},{14,16},{16,18},{18... | collective-permute-start | bytes 393224 | tf_op jit(solution)/shard_map/ppermute | solution.py:14
  290.0 10.1 %collective-permute-start.15 = (bf16[32,2,256]{2,0,1:T(8,128)(2,1)}, bf16[32,2,256]{2,0,1:T(8,128)(2,1)}, u32[]{:S(2)}, u32[]{:S(2)}) collective-permute-start(bf16[32,2,256]{2,0,1:T(8,128)(2,1)} %collective-permute-done.13), channel_id=1, source_target_pairs={{0,2},{2,4},{4,6},{6,8},{8,10},{10,12},{12,14},{14,16},{16,18},{18... | collective-permute-start | bytes 98312 | tf_op jit(solution)/shard_map/ppermute | solution.py:190
  291.3 8.9 %collective-permute-start.16 = (bf16[32,2,256]{2,0,1:T(8,128)(2,1)}, bf16[32,2,256]{2,0,1:T(8,128)(2,1)}, u32[]{:S(2)}, u32[]{:S(2)}) collective-permute-start(bf16[32,2,256]{2,0,1:T(8,128)(2,1)} %collective-permute-done.14), channel_id=1, source_target_pairs={{0,30},{2,0},{4,2},{6,4},{8,6},{10,8},{12,10},{14,12},{16,14},{18,... | collective-permute-start | bytes 98312 | tf_op jit(solution)/shard_map/ppermute | solution.py:193
  300.1 7.8 %collective-permute-start.17 = (bf16[32,2,256]{2,0,1:T(8,128)(2,1)}, bf16[32,2,256]{2,0,1:T(8,128)(2,1)S(1)}, u32[]{:S(2)}, u32[]{:S(2)}) collective-permute-start(bf16[32,2,256]{2,0,1:T(8,128)(2,1)} %collective-permute-done.15), channel_id=1, source_target_pairs={{0,2},{2,4},{4,6},{6,8},{8,10},{10,12},{12,14},{14,16},{16,18},{18... | collective-permute-start | bytes 98312 | tf_op jit(solution)/shard_map/ppermute | solution.py:190
  300.2 7.7 %collective-permute-start.18 = (bf16[32,2,256]{2,0,1:T(8,128)(2,1)}, bf16[32,2,256]{2,0,1:T(8,128)(2,1)S(1)}, u32[]{:S(2)}, u32[]{:S(2)}) collective-permute-start(bf16[32,2,256]{2,0,1:T(8,128)(2,1)} %collective-permute-done.16), channel_id=1, source_target_pairs={{0,30},{2,0},{4,2},{6,4},{8,6},{10,8},{12,10},{14,12},{16,14},{18,... | collective-permute-start | bytes 98312 | tf_op jit(solution)/shard_map/ppermute | solution.py:193
  315.4 7.5 %collective-permute-start.22 = (bf16[32,2,256]{2,0,1:T(8,128)(2,1)S(1)}, bf16[32,2,256]{2,0,1:T(8,128)(2,1)S(1)}, u32[]{:S(2)}, u32[]{:S(2)}) collective-permute-start(bf16[32,2,256]{2,0,1:T(8,128)(2,1)S(1)} %collective-permute-done.20), channel_id=1, source_target_pairs={{0,30},{2,0},{4,2},{6,4},{8,6},{10,8},{12,10},{14,12},{16,14},{18,... | collective-permute-start | bytes 98312 | tf_op jit(solution)/shard_map/ppermute | solution.py:193
  (70 other events, 427.0 us)
Sparse Core Ops, SparseCore 0:
  331.7 3.5 reduce-scatter.1
